TPU v7x, 32 devices: a whole 2x2x4 slice. The times are simulated.
32 devices in a mesh: dp: 4 (over y, core), space: 8 (over z, x).
Axes of the slice: x: 2, y: 2, z: 4, core: 2. Of those that a mesh axis runs over, the one named last changes fastest.
Arguments:
- activations: bfloat16 [2, 4, 8, 16, 32, 768], P(None, 'dp', None, 'space'), may hold values from -60 to 60
- out_grads: bfloat16 [2, 4, 8, 16, 32, 768], P(None, 'dp', None, 'space'), may hold values from -6 to 6
- omega: bfloat16 [768, 128], replicated, may hold values from -0.21875 to 0.21875
Outputs:
- basis: float32 [2, 20736, 128], P(None, ('dp', 'space'))
All inputs are finite; a program needn't handle non-finite values.
Results may differ from a plain program's by a relative error of at most 0.0033.
Values may be sent and summed in bfloat16 or wider, within the bound.
No kernel may reach another device: no remote copies, remote signals or barrier semaphores. Data moves between devices by JAX's collectives and lax.ppermute only.
A program may use at most 128 MiB of HBM per device.

v0:
```python
import math

import jax
import jax.numpy as jnp
from jax import lax
from jax.sharding import PartitionSpec as P


def with_halo(value, sides, width):
    for axis, dim in sides:
        count, length = (lax.axis_size(axis), value.shape[dim])
        up = [(i, (i + 1) % count) for i in range(count - 1)]
        down = [(j, i) for i, j in up]
        last = lax.slice_in_dim(value, length - width, length, axis=dim)
        initial = lax.slice_in_dim(value, 0, width, axis=dim)
        before = lax.ppermute(last, axis, up)
        after = lax.ppermute(initial, axis, down)
        value = jnp.concatenate([before, value, after], axis=dim)
    return value


def solve_layer(lower, block_rows):
    return jax.scipy.linalg.solve_triangular(lower, block_rows.T, lower=True).T


def shards(activations, out_grads, omega):
    layer_count, clips, frames, height, widths, channels = activations.shape
    rank_cols = omega.shape[1]
    grads_flat = out_grads.reshape(-1, channels)
    sketched = jnp.dot(grads_flat, omega, preferred_element_type=jnp.float32).astype(jnp.bfloat16)
    sketched = sketched.reshape(layer_count, clips, frames, height, widths, rank_cols)
    padding = ((0, 0), (0, 0), (1, 1), (0, 0), (1, 1), (0, 0))
    per_layer = []
    extended = with_halo(sketched, (("space", 3),), 1)
    extended = jnp.pad(extended, padding)
    for layer in range(layer_count):
        shifted = []
        for along_t in range(3):
            for along_h in range(3):
                for along_w in range(3):
                    window = extended[
                        layer,
                        :,
                        2 - along_t : 2 - along_t + frames,
                        2 - along_h : 2 - along_h + height,
                        2 - along_w : 2 - along_w + widths,
                        :,
                    ]
                    shifted.append(window.reshape(-1, rank_cols))
        shifted = jnp.stack(shifted, axis=1)
        inputs_flat = activations[layer].reshape(-1, channels)
        product = jnp.einsum(
            "nc,nkr->kcr", inputs_flat, shifted, preferred_element_type=jnp.float32
        )
        per_layer.append(product.reshape(-1, rank_cols))
    partial_sketch = jnp.stack(per_layer)
    rows_block = lax.psum_scatter(partial_sketch, ("dp", "space"), scatter_dimension=1, tiled=True)
    gram_local = jnp.einsum("lnr,lns->lrs", rows_block, rows_block, precision=lax.Precision.HIGHEST)
    total = lax.psum(gram_local, ("dp", "space"))
    lower = jnp.linalg.cholesky(total)
    basis = jax.vmap(solve_layer)(lower, rows_block)
    return basis * math.sqrt(27 * channels)


def solution(mesh):
    return jax.shard_map(
        shards,
        mesh=mesh,
        in_specs=(
            P(None, "dp", None, "space", None, None),
            P(None, "dp", None, "space", None, None),
            P(),
        ),
        out_specs=P(None, ("dp", "space"), None),
        check_vma=False,
    )
```

profile of v0, /device:TPU:0, one launch (start us, length us, event | category | flops | bytes accessed | tf_op | source)
XLA Modules:
  0.0 491.7 jit_solution(17926732929990991419)
XLA Ops:
  6.5 0.0 copy-start
  6.5 0.0 reduce-scatter.2.cloned.1.call-start
  6.5 1.4 copy-done
  7.9 0.0 copy-start.3
  7.9 1.6 convolution_convert_fusion
  9.6 4.9 collective-permute-start
  14.5 1.3 collective-permute-start.1
  15.8 0.0 copy-done.3
  15.8 0.1 fusion.10
  15.9 1.3 collective-permute-done
  17.2 4.1 collective-permute-done.1
  21.3 0.3 select_maximum_fusion
  21.6 0.6 fusion.12
  22.2 0.4 fusion.11
  22.6 0.2 fusion.13
  23.7 0.0 copy-start.2
  24.0 1.5 copy-done.2
  25.5 5.6 %convolution_bitcast_fusion.1 = f32[27,768,128]{1,2,0:T(8,128)} fusion(bf16[512,27,128]{2,0,1:T(8,128)(2,1)S(1)} %constant_dynamic-update-slice_fusion, bf16[512,768,1]{1,0,2:T(8,128)(2,1)S(1)} %bitcast.105), kind=kOutput, calls=%fused_computation.2 | convolution fusion | flops 2717908992 | bytes 14942208 | tf_op jit(solution)/shard_map/nc,nkr->kcr/dot_general | solution.py:52
  31.2 11.5 %copy.32 = f32[27,768,128]{2,1,0:T(8,128)} copy(f32[27,768,128]{1,2,0:T(8,128)} %convolution_bitcast_fusion.1) | data formatting | bytes 21233664 | tf_op jit(solution)/shard_map/nc,nkr->kcr/transpose | solution.py:52
  42.7 0.7 constant_dynamic-update-slice_fusion.37
  43.4 0.7 constant_dynamic-update-slice_fusion.36
  44.1 0.7 constant_dynamic-update-slice_fusion.35
  44.7 0.7 constant_dynamic-update-slice_fusion.34
  45.4 0.7 constant_dynamic-update-slice_fusion.33
  46.1 0.7 constant_dynamic-update-slice_fusion.32
  46.7 0.7 constant_dynamic-update-slice_fusion.31
  47.4 0.7 constant_dynamic-update-slice_fusion.30
  48.1 0.7 constant_dynamic-update-slice_fusion.29
  48.7 0.7 constant_dynamic-update-slice_fusion.28
  49.4 0.7 constant_dynamic-update-slice_fusion.27
  50.0 0.7 constant_dynamic-update-slice_fusion.26
  50.7 9.0 %convolution_bitcast_fusion = f32[27,768,128]{1,2,0:T(8,128)} fusion(bf16[512,27,128]{2,0,1:T(8,128)(2,1)} %constant_dynamic-update-slice_fusion.26, bf16[512,768,1]{1,0,2:T(8,128)(2,1)S(1)} %bitcast.104), kind=kOutput, calls=%fused_computation.1 | convolution fusion | flops 2717908992 | bytes 14942208 | tf_op jit(solution)/shard_map/nc,nkr->kcr/dot_general | solution.py:52
  59.7 11.6 %copy.34 = f32[27,768,128]{2,1,0:T(8,128)} copy(f32[27,768,128]{1,2,0:T(8,128)} %convolution_bitcast_fusion) | data formatting | bytes 21233664 | tf_op jit(solution)/shard_map/nc,nkr->kcr/transpose | solution.py:52
  71.3 15.9 %pad_maximum_fusion = f32[2,20736,128]{2,1,0:T(8,128)} fusion(f32[1,20736,128]{2,1,0:T(8,128)} %bitcast.100, f32[1,20736,128]{2,1,0:T(8,128)} %bitcast.99), kind=kLoop, calls=%fused_computation | loop fusion | flops 5308416 | bytes 42467328 | tf_op jit(solution)/shard_map/stack | solution.py:56
  87.1 0.0 reduce-scatter.2.cloned.1.call-update
  87.2 0.0 copy-start.1
  87.2 0.2 all-reduce.3.cloned.1.call-start
  87.4 219.5 %reduce-scatter.2.cloned.1.call-done = f32[2,648,128]{2,1,0:T(8,128)} async-done(((f32[2,20736,128]{2,1,0:T(8,128)}), f32[2,648,128]{2,1,0:T(8,128)}) %reduce-scatter.2.cloned.1.call-update) | async-done | bytes 663568 | tf_op jit(solution)/shard_map/reduce_scatter | solution.py:57
  306.9 3.5 fusion.15
  310.4 0.0 all-reduce.3.cloned.1.call-update
  310.4 126.0 %all-reduce.3.cloned.1.call-done = f32[2,128,128]{1,2,0:T(8,128)} async-done(((f32[2,128,128]{1,2,0:T(8,128)}), f32[2,128,128]{1,2,0:T(8,128)}) %all-reduce.3.cloned.1.call-update) | async-done | bytes 131088 | tf_op jit(solution)/shard_map/psum | solution.py:59
  436.4 1.0 copy.36
  437.4 0.9 fusion.9
  438.4 23.5 %custom-call.8 = f32[2,128,128]{2,1,0:T(8,128)S(1)} custom-call(f32[2,128,128]{2,1,0:T(8,128)S(1)} %fusion.9), custom_call_target="Cholesky" | custom-call | tf_op jit(solution)/shard_map/jit(cholesky)/cholesky | solution.py:60
  461.9 0.1 compare_reduce_fusion
  462.0 0.1 select_bitcast_fusion
  462.1 19.7 %custom-call.9 = f32[2,1,128,128]{2,3,1,0:T(8,128)S(1)} custom-call(f32[2,1,128,128]{3,2,1,0:T(8,128)S(1)} %select_bitcast_fusion), custom_call_target="InvertDiagBlocksLowerTriangular" | custom-call | tf_op jit(solution)/shard_map/vmap(jit(_solve_triangular))/triangular_solve | solution.py:23
  481.8 3.1 convolution_multiply_fusion
  484.9 0.0 copy-done.1
  (45 shorter events, 0.9 us)
Async XLA Ops:
  6.5 1.4 copy-start
  6.5 300.4 %reduce-scatter.2.cloned.1.call-start = ((), (), s32[]{:S(2)}) async-start(), calls=%async_computation.1 | async-start | bytes 21897216 | tf_op jit(solution)/shard_map/reduce_scatter | solution.py:57
  7.9 7.8 %copy-start.3 = (bf16[2,1,8,2,32,768]{5,4,3,2,1,0:T(8,128)(2,1)S(1)}, bf16[2,1,8,2,32,768]{5,4,3,2,1,0:T(8,128)(2,1)}, u32[]{:S(2)}) copy-start(bf16[2,1,8,2,32,768]{5,4,3,2,1,0:T(8,128)(2,1)} %param.3) | copy-start | bytes 4718596
  9.6 7.6 %collective-permute-start = (bf16[2,1,8,1,32,128]{5,4,3,2,1,0:T(8,128)(2,1)S(1)}, bf16[2,1,8,1,32,128]{5,4,3,2,1,0:T(8,128)(2,1)S(1)}, u32[]{:S(2)}, u32[]{:S(2)}) collective-permute-start(bf16[2,1,8,1,32,128]{5,4,3,2,1,0:T(8,128)(2,1)S(1)} %get-tuple-element.63), channel_id=1, source_target_pairs={{0,1},{1,2},{2,3},{3,4},{4,5},{5,6},{6,7},{8,9},{9,10},{10,11},{11... | collective-permute-start | bytes 393224 | tf_op jit(solution)/shard_map/ppermute | solution.py:16
  14.5 6.9 %collective-permute-start.1 = (bf16[2,1,8,1,32,128]{5,4,3,2,1,0:T(8,128)(2,1)S(1)}, bf16[2,1,8,1,32,128]{5,4,3,2,1,0:T(8,128)(2,1)S(1)}, u32[]{:S(2)}, u32[]{:S(2)}) collective-permute-start(bf16[2,1,8,1,32,128]{5,4,3,2,1,0:T(8,128)(2,1)S(1)} %get-tuple-element.64), channel_id=1, source_target_pairs={{1,0},{2,1},{3,2},{4,3},{5,4},{6,5},{7,6},{9,8},{10,9},{11,10},{12... | collective-permute-start | bytes 393224 | tf_op jit(solution)/shard_map/ppermute | solution.py:17
  23.7 1.9 copy-start.2
  87.2 397.7 %copy-start.1 = (bf16[2,1,8,2,32,768]{5,4,3,2,1,0:T(8,128)(2,1)S(1)}, bf16[2,1,8,2,32,768]{5,4,3,2,1,0:T(8,128)(2,1)}, u32[]{:S(2)}) copy-start(bf16[2,1,8,2,32,768]{5,4,3,2,1,0:T(8,128)(2,1)} %param.4) | copy-start | bytes 4718596
  87.2 349.3 %all-reduce.3.cloned.1.call-start = ((), (), s32[]{:S(2)}) async-start(), calls=%async_computation.2 | async-start | bytes 262144 | tf_op jit(solution)/shard_map/psum | solution.py:59
Sparse Core Ops, SparseCore 0:
  87.3 219.6 reduce-scatter.1
  312.5 123.9 all-reduce.2
where the time goes:
time: 492 us
  waiting for transfers between devices  351 us (71%)
  other arithmetic  60.5 us (12%)
  local copies, waits for them, and re-layouts  37.2 us (8%)
  matrix products  22.8 us (5%)
  between operations  13.9 us (3%)
  starting transfers between devices  6.39 us (1%)
    reduce_scatter x1, waiting for transfers between devices, shards(): lax.psum_scatter(partial_sketch, ('dp', 'space'), scatter_dimension=1, ti...  220 us
    psum x1, waiting for transfers between devices, shards(): total = lax.psum(gram_local, ('dp', 'space'))  126 us
    another operation x4, other arithmetic, shards(): lower = jnp.linalg.cholesky(total)  23.6 us
    transpose x2, local copies, waits for them, and re-layouts, shards(): jnp.einsum('nc,nkr->kcr', inputs_flat, shifted, preferred_element_type=jn...  23.1 us
    another operation x3, other arithmetic, solve_layer(): return jax.scipy.linalg.solve_triangular(lower, block_rows.T, lower=True).T  19.8 us
    another operation x1, other arithmetic, shards(): partial_sketch = jnp.stack(per_layer)  15.9 us
    dot_general x2, matrix products, shards(): jnp.einsum('nc,nkr->kcr', inputs_flat, shifted, preferred_element_type=jn...  14.6 us
    unnamed x58, local copies, waits for them, and re-layouts  11 us
  transfers between devices with their start and end apart: 4, of which 4 were waited for; matrix products, arithmetic and copies ran while one was open for 0% of the time, Pallas kernels for 0%

commit v1 on v0

v1 whole, which is shorter than its diff:
```python
import functools
import math

import jax
import jax.numpy as jnp
from jax import lax
from jax.experimental import pallas as pl
from jax.experimental.pallas import tpu as pltpu
from jax.sharding import PartitionSpec as P

AXES = ("dp", "space")
F32, BF16 = jnp.float32, jnp.bfloat16
HIGHEST = lax.Precision.HIGHEST


def swap(value, mask, total):
    return lax.ppermute(value, AXES, [(d, d ^ mask) for d in range(total)])


def halo(value, axis, dim):
    count, length = lax.axis_size(axis), value.shape[dim]
    up = [(i, i + 1) for i in range(count - 1)]
    before = lax.ppermute(lax.slice_in_dim(value, length - 1, length, axis=dim), axis, up)
    after = lax.ppermute(lax.slice_in_dim(value, 0, 1, axis=dim), axis, [(j, i) for i, j in up])
    return jnp.concatenate([before, value, after], axis=dim)


def product_kernel(frames, height, widths, rank, act_ref, sk_ref, out_ref, act_t, wide):
    step = pl.program_id(0)

    @pl.when(step == 0)
    def _():
        act_t[...] = act_ref[...].T
        zero = jnp.zeros((height + 2, widths, 3 * rank), BF16)
        wide[0] = zero
        wide[frames + 1] = zero
        rows = frames * (height + 2) * widths
        flat = sk_ref[...].astype(F32).reshape(rows, rank)
        at = lax.rem(lax.broadcasted_iota(jnp.int32, (rows, rank), 0), widths)
        later = jnp.where(at == widths - 1, 0.0, pltpu.roll(flat, rows - 1, 0))
        earlier = jnp.where(at == 0, 0.0, pltpu.roll(flat, 1, 0))
        shape = (frames, height + 2, widths, rank)
        wide[1 : frames + 1, :, :, 0:rank] = later.astype(BF16).reshape(shape)
        wide[1 : frames + 1, :, :, rank : 2 * rank] = sk_ref[...]
        wide[1 : frames + 1, :, :, 2 * rank :] = earlier.astype(BF16).reshape(shape)

    along_t, along_h = step // 3, lax.rem(step, 3)
    window = wide[pl.ds(2 - along_t, frames), pl.ds(2 - along_h, height)]
    window = window.reshape(frames * height * widths, 3 * rank)
    made = jnp.dot(act_t[...], window, preferred_element_type=F32)
    for c in range(3):
        out_ref[c] = made[:, c * rank : (c + 1) * rank]


def product(act, extended):
    frames, rows, widths, rank = extended.shape
    height, channels = rows - 2, act.shape[-1]
    positions = frames * height * widths
    return pl.pallas_call(
        functools.partial(product_kernel, frames, height, widths, rank),
        grid=(9,),
        in_specs=[
            pl.BlockSpec((positions, channels), lambda s: (0, 0)),
            pl.BlockSpec((frames, rows, widths, rank), lambda s: (0, 0, 0, 0)),
        ],
        out_specs=pl.BlockSpec((3, channels, rank), lambda s: (s, 0, 0)),
        out_shape=jax.ShapeDtypeStruct((27, channels, rank), F32),
        scratch_shapes=[
            pltpu.VMEM((channels, positions), BF16),
            pltpu.VMEM((frames + 2, rows, widths, 3 * rank), BF16),
        ],
        compiler_params=pltpu.CompilerParams(vmem_limit_bytes=40 * 2**20),
        cost_estimate=pl.CostEstimate(
            flops=2 * 27 * positions * channels * rank,
            bytes_accessed=27 * channels * rank * 4 + positions * channels * 2,
            transcendentals=0,
        ),
        name="product",
    )(act.reshape(positions, channels), extended)


def inverse_kernel(size, gram_ref, out_ref, work):
    eye = lax.broadcasted_iota(jnp.int32, (size, size), 0) == lax.broadcasted_iota(jnp.int32, (size, size), 1)
    work[:, :size] = gram_ref[...]
    work[:, size:] = eye.astype(F32)
    sub = lax.broadcasted_iota(jnp.int32, (8, 1), 0)
    for start in range(0, size, 8):
        rows = work[start : start + 8, :]
        cols = [jnp.broadcast_to(rows[:, start + r : start + r + 1], (8, size)) for r in range(8)]
        for r in range(8):
            scale = lax.rsqrt(cols[r][r : r + 1, :])
            below = jnp.where(sub > r, cols[r] * scale, 0.0)
            for c in range(r + 1, 8):
                cols[c] = cols[c] - below * (cols[c][r : r + 1, :] * scale)
            both = jnp.concatenate([scale, scale], axis=1)
            row = rows[r : r + 1, :] * both
            rows = jnp.where(sub == r, row, rows - jnp.concatenate([below, below], axis=1) * row)
        out_ref[start : start + 8, :] = rows[:, size:]
        if start + 8 < size:
            left = rows[:, start + 8 : size] if (start + 8) % size == 0 else rows[:, :size]
            update = lax.dot_general(
                left, rows, (((0,), (0,)), ((), ())), precision=HIGHEST, preferred_element_type=F32
            )
            work[start + 8 :, :] = work[start + 8 :, :] - update[start + 8 :, :]


def inverse_of_factor(gram):
    size = gram.shape[-1]
    return pl.pallas_call(
        functools.partial(inverse_kernel, size),
        out_shape=jax.ShapeDtypeStruct((size, size), F32),
        scratch_shapes=[pltpu.VMEM((size, 2 * size), F32)],
        name="inverse",
    )(gram)


def pick(value, index, axis):
    return lax.dynamic_index_in_dim(value, index, axis, keepdims=False)


def halve(value, axis, own, mask, total):
    sent = pick(value, 1 - own, axis).astype(BF16)
    return pick(value, own, axis) + swap(sent, mask, total).astype(F32)


def scatter_layer(partial, bits, total):
    rank = partial.shape[-1]
    rows = partial.shape[0] * partial.shape[1] // total
    count = len(bits)
    core_at = count - 1 - (lax.axis_size("space").bit_length() - 1)
    view = partial.reshape((2,) * count + (rows, rank))
    masks = [1 << (count - 1 - i) for i in range(count)]
    if count == 5 and core_at == 1:
        y, _, zh, zl, x = bits
        my, mc, mzh, mzl, mx = masks
        view = halve(view, 1, bits[1], mc, total)
        one, two = view[:, 0], view[:, 1]
        one = halve(one, 2, x, mx, total)
        two = halve(two, 0, y, my, total)
        one = halve(one, 0, y, my, total)
        two = halve(two, 1, x, mx, total)
        z = 2 * zh + zl
        both = jnp.stack([one, two]).reshape(4, rows, rank)
        got = [swap(pick(both, z ^ m, 0).astype(BF16), m * mzl, total) for m in (1, 2, 3)]
        return pick(both, z, 0) + (got[0].astype(F32) + got[1].astype(F32) + got[2].astype(F32))
    order = [core_at] + [i for i in range(count) if i != core_at]
    left = list(range(count))
    for i in order:
        view = halve(view, left.index(i), bits[i], masks[i], total)
        left.remove(i)
    return view


def shards(activations, out_grads, omega):
    layer_count, clips, frames, height, widths, channels = activations.shape
    rank = omega.shape[1]
    total = lax.axis_size("dp") * lax.axis_size("space")
    count = total.bit_length() - 1
    me = lax.axis_index("dp") * lax.axis_size("space") + lax.axis_index("space")
    bits = [(me >> (count - 1 - i)) & 1 for i in range(count)]
    core_mask = lax.axis_size("space")
    core = lax.axis_index("dp") & 1

    sketched = jnp.dot(out_grads.reshape(-1, channels), omega, preferred_element_type=F32).astype(BF16)
    sketched = sketched.reshape(layer_count, frames, height, widths, rank)
    extended = halo(sketched, "space", 2)
    blocks = []
    for layer in range(layer_count):
        partial = product(activations[layer], extended[layer])
        blocks.append(scatter_layer(partial, bits, total))
    rows = jnp.stack(blocks)
    gram = jnp.einsum("lnr,lns->lrs", rows, rows, precision=HIGHEST)
    mine = pick(gram, core, 0) + swap(pick(gram, 1 - core, 0), core_mask, total)
    for i in range(count):
        mask = 1 << i
        if mask != core_mask:
            mine = mine + swap(mine, mask, total)
    inverse = inverse_of_factor(mine)
    other = swap(inverse, core_mask, total)
    inverses = [jnp.where(core == layer, inverse, other) for layer in range(2)]
    scale = math.sqrt(27 * channels)
    basis = [jnp.dot(rows[i], inverses[i].T, precision=HIGHEST) * scale for i in range(2)]
    return jnp.stack(basis)


def solution(mesh):
    return jax.shard_map(
        shards,
        mesh=mesh,
        in_specs=(
            P(None, "dp", None, "space", None, None),
            P(None, "dp", None, "space", None, None),
            P(),
        ),
        out_specs=P(None, ("dp", "space"), None),
        check_vma=False,
    )
```

time: 492 us -> 153 us (0.31)
  waiting for transfers between devices: 351 us -> 65.7 us
  other arithmetic: 60.5 us -> 9 us
  starting transfers between devices: 6.39 us -> 34.5 us
  local copies, waits for them, and re-layouts: 37.2 us -> 15 us
  Pallas kernels: 0 us -> 21.3 us
  matrix products: 22.8 us -> 6.68 us
  between operations: 13.9 us -> 0.39 us
    reduce_scatter x1 -> x0, waiting for transfers between devices: 220 us -> none  [shards(): lax.psum_scatter(partial_sketch, ('dp', 'space'), scatter_dimension=1, ti...]
    psum x1 -> x0, waiting for transfers between devices: 126 us -> none  [shards(): total = lax.psum(gram_local, ('dp', 'space'))]
    ppermute x2 -> x24, waiting for transfers between devices: 5.41 us -> 65.7 us  [the longest x22 60.3 us: swap(): return lax.ppermute(value, AXES, [(d, d ^ mask) for d in range(total)])]
    another operation x8 -> x9, other arithmetic: 59.3 us -> 1.54 us  [the longest x1 0.92 us: shards(): return jnp.stack(basis)]
    ppermute x2 -> x24, starting transfers between devices: 6.17 us -> 34.5 us  [the longest x22 28.4 us: swap(): return lax.ppermute(value, AXES, [(d, d ^ mask) for d in range(total)])]
    transpose x2 -> x0, local copies, waits for them, and re-layouts: 23.1 us -> none  [shards(): jnp.einsum('nc,nkr->kcr', inputs_flat, shifted, preferred_element_type=jn...]
    pallas_call x0 -> x3, Pallas kernels: none -> 21.3 us  [the longest x2 11.9 us: product(): pl.pallas_call(functools.partial(product_kernel, frames, height, widths,...]
    dot_general x4, matrix products: 19.7 us -> 6.68 us  [the longest x2 3.58 us: shards(): jnp.dot(rows[i], inverses[i].T, precision=HIGHEST) * scale]
  transfers between devices with their start and end apart: 4 -> 24, of which waited for: 4 -> 17; matrix products, arithmetic and copies ran while one was open for 0% -> 7% of each run, Pallas kernels for 0% -> 4%
where the time goes in v1:
time: 153 us
  waiting for transfers between devices  65.7 us (43%)
  starting transfers between devices  34.5 us (23%)
  Pallas kernels  21.3 us (14%)
  local copies, waits for them, and re-layouts  15 us (10%)
  other arithmetic  9 us (6%)
  matrix products  6.68 us (4%)
    ppermute x22, waiting for transfers between devices, swap(): return lax.ppermute(value, AXES, [(d, d ^ mask) for d in range(total)])  60.3 us
    ppermute x22, starting transfers between devices, swap(): return lax.ppermute(value, AXES, [(d, d ^ mask) for d in range(total)])  28.4 us
    pallas_call x2, Pallas kernels, product(): pl.pallas_call(functools.partial(product_kernel, frames, height, widths,...  11.9 us
    pallas_call x1, Pallas kernels, inverse_of_factor(): pl.pallas_call(functools.partial(inverse_kernel, size), out_shape=jax.Sha...  9.43 us
    unnamed x24, local copies, waits for them, and re-layouts  9.38 us
    add x6, other arithmetic, halve(): return pick(value, own, axis) + swap(sent, mask, total).astype(F32)  6.73 us
    ppermute x1, starting transfers between devices, halo(): lax.ppermute(lax.slice_in_dim(value, length - 1, length, axis=dim), axis,...  4.88 us
    convert_element_type x10, local copies, waits for them, and re-layouts, halve(): sent = pick(value, 1 - own, axis).astype(BF16)  4.62 us
  transfers between devices with their start and end apart: 24, of which 17 were waited for; matrix products, arithmetic and copies ran while one was open for 7% of the time, Pallas kernels for 4%

profile of v1, /device:TPU:0, one launch (start us, length us, event | category | flops | bytes accessed | tf_op | source)
XLA Modules:
  0.0 152.7 jit_solution(13308752780826295415)
XLA Ops:
  0.0 1.4 copy-done
  1.4 1.6 %convolution_convert_fusion = bf16[1024,128]{1,0:T(8,128)(2,1)S(1)} fusion(bf16[1024,768]{1,0:T(8,128)(2,1)S(1)} %bitcast.116, bf16[768,128]{1,0:T(8,128)(2,1)} %param.5), kind=kOutput, calls=%fused_computation.16 | convolution fusion | flops 201457664 | bytes 2031616 | tf_op jit(solution)/shard_map/dot_general | solution.py:164
  3.1 4.9 %collective-permute-start = (bf16[2,8,1,32,128]{4,3,2,1,0:T(8,128)(2,1)S(1)}, bf16[2,8,1,32,128]{4,3,2,1,0:T(8,128)(2,1)S(1)}, u32[]{:S(2)}, u32[]{:S(2)}) collective-permute-start(bf16[2,8,1,32,128]{4,3,2,1,0:T(8,128)(2,1)S(1)} %get-tuple-element.19), channel_id=1, source_target_pairs={{0,1},{1,2},{2,3},{3,4},{4,5},{5,6},{6,7},{8,9},{9,10},{10,11},{11... | collective-permute-start | bytes 393224 | tf_op jit(solution)/shard_map/ppermute | solution.py:23
  7.9 1.3 collective-permute-start.1
  9.3 0.1 fusion.35
  9.4 1.3 collective-permute-done
  10.7 4.1 %collective-permute-done.1 = bf16[2,8,1,32,128]{4,3,2,1,0:T(8,128)(2,1)S(1)} collective-permute-done((bf16[2,8,1,32,128]{4,3,2,1,0:T(8,128)(2,1)S(1)}, bf16[2,8,1,32,128]{4,3,2,1,0:T(8,128)(2,1)S(1)}, u32[]{:S(2)}, u32[]{:S(2)}) %collective-permute-start.1) | collective-permute-done | bytes 131104 | tf_op jit(solution)/shard_map/ppermute | solution.py:24
  14.9 5.8 %product.2 = f32[27,768,128]{2,1,0:T(8,128)S(1)} custom-call(bf16[512,768]{1,0:T(8,128)(2,1)S(1)} %bitcast.124, bf16[8,4,32,128]{3,2,1,0:T(8,128)(2,1)S(1)} %get-tuple-element.17.sk_ref), custom_call_target="tpu_custom_call" | custom-call | flops 2717908992 | bytes 11403264 | tf_op jit(solution)/shard_map/product/pallas_call | solution.py:59
  20.8 2.2 %fusion = bf16[2,2,2,2,648,128]{5,4,3,2,1,0:T(8,128)(2,1)} fusion(f32[2,2,2,2,2,648,128]{6,5,4,3,2,1,0:T(8,128)S(1)} %bitcast.121, s32[]{:T(128)S(6)} %select_n.76), kind=kLoop, calls=%fused_computation.4 | loop fusion | bytes 5308420 | tf_op jit(solution)/shard_map/convert_element_type | solution.py:122
  22.9 2.5 %copy-done.3 = f32[27,768,128]{2,1,0:T(8,128)} copy-done((f32[27,768,128]{2,1,0:T(8,128)}, f32[27,768,128]{2,1,0:T(8,128)S(1)}, u32[]{:S(2)}) %copy-start.3) | copy-done | bytes 10616856
  25.5 6.0 %product.3 = f32[27,768,128]{2,1,0:T(8,128)S(1)} custom-call(bf16[512,768]{1,0:T(8,128)(2,1)S(1)} %bitcast.123, bf16[8,4,32,128]{3,2,1,0:T(8,128)(2,1)S(1)} %get-tuple-element.18.sk_ref), custom_call_target="tpu_custom_call" | custom-call | flops 2717908992 | bytes 11403264 | tf_op jit(solution)/shard_map/product/pallas_call | solution.py:59
  31.5 4.1 %copy-done.2 = f32[27,768,128]{2,1,0:T(8,128)} copy-done((f32[27,768,128]{2,1,0:T(8,128)}, f32[27,768,128]{2,1,0:T(8,128)S(1)}, u32[]{:S(2)}) %copy-start.2) | copy-done | bytes 10616856
  35.6 1.9 %fusion.1 = bf16[2,2,2,2,648,128]{5,4,3,2,1,0:T(8,128)(2,1)} fusion(f32[2,2,2,2,2,648,128]{6,5,4,3,2,1,0:T(8,128)S(1)} %bitcast.117, s32[]{:T(128)S(6)} %select_n.76), kind=kLoop, calls=%fused_computation.5 | loop fusion | bytes 5308420 | tf_op jit(solution)/shard_map/convert_element_type | solution.py:122
  37.5 3.9 %bitcast_add_fusion.1 = f32[2,2,2,2,648,128]{5,4,3,2,1,0:T(8,128)S(1)} fusion(bf16[2,2,2,2,648,128]{5,4,3,2,1,0:T(8,128)(2,1)} %collective-permute-done.2, f32[2,2,2,2,2,648,128]{6,5,4,3,2,1,0:T(8,128)} %bitcast.122, s32[]{:T(128)S(6)} %select_n.75), kind=kLoop, calls=%fused_computation.1 | loop fusion | flops 2654208 | bytes 13271044 | tf_op jit(solution)/shard_map/add | solution.py:123
  41.4 0.3 fusion.33
  41.7 0.1 fusion.6
  41.8 2.5 %collective-permute-start.3 = (bf16[2,2,648,128]{3,2,1,0:T(8,128)(2,1)S(1)}, bf16[2,2,648,128]{3,2,1,0:T(8,128)(2,1)S(1)}, u32[]{:S(2)}, u32[]{:S(2)}) collective-permute-start(bf16[2,2,648,128]{3,2,1,0:T(8,128)(2,1)S(1)} %fusion.6), channel_id=1, source_target_pairs={{0,1},{1,0},{2,3},{3,2},{4,5},{5,4},{6,7},{7,6},{8,9},{9,8},{10,11... | collective-permute-start | bytes 1990664 | tf_op jit(solution)/shard_map/ppermute | solution.py:17
  44.5 1.6 %collective-permute-start.5 = (bf16[2,2,648,128]{3,2,1,0:T(8,128)(2,1)S(1)}, bf16[2,2,648,128]{3,2,1,0:T(8,128)(2,1)S(1)}, u32[]{:S(2)}, u32[]{:S(2)}) collective-permute-start(bf16[2,2,648,128]{3,2,1,0:T(8,128)(2,1)S(1)} %fusion.4), channel_id=1, source_target_pairs={{0,16},{1,17},{2,18},{3,19},{4,20},{5,21},{6,22},{7,23},{8,24},{9,... | collective-permute-start | bytes 1990664 | tf_op jit(solution)/shard_map/ppermute | solution.py:17
  46.1 2.3 %bitcast_add_fusion = f32[2,2,2,2,648,128]{5,4,3,2,1,0:T(8,128)S(1)} fusion(bf16[2,2,2,2,648,128]{5,4,3,2,1,0:T(8,128)(2,1)} %collective-permute-done.10, f32[2,2,2,2,2,648,128]{6,5,4,3,2,1,0:T(8,128)S(1)} %bitcast.120, s32[]{:T(128)S(6)} %select_n.75), kind=kLoop, calls=%fused_computation | loop fusion | flops 2654208 | bytes 13271044 | tf_op jit(solution)/shard_map/add | solution.py:123
  48.4 0.3 fusion.34
  48.7 0.1 fusion.7
  48.8 0.5 collective-permute-start.11
  49.5 1.6 %collective-permute-start.13 = (bf16[2,2,648,128]{3,2,1,0:T(8,128)(2,1)S(1)}, bf16[2,2,648,128]{3,2,1,0:T(8,128)(2,1)S(1)}, u32[]{:S(2)}, u32[]{:S(2)}) collective-permute-start(bf16[2,2,648,128]{3,2,1,0:T(8,128)(2,1)S(1)} %fusion.5), channel_id=1, source_target_pairs={{0,16},{1,17},{2,18},{3,19},{4,20},{5,21},{6,22},{7,23},{8,24},{9,... | collective-permute-start | bytes 1990664 | tf_op jit(solution)/shard_map/ppermute | solution.py:17
  51.0 9.1 %collective-permute-done.3 = bf16[2,2,648,128]{3,2,1,0:T(8,128)(2,1)S(1)} collective-permute-done((bf16[2,2,648,128]{3,2,1,0:T(8,128)(2,1)S(1)}, bf16[2,2,648,128]{3,2,1,0:T(8,128)(2,1)S(1)}, u32[]{:S(2)}, u32[]{:S(2)}) %collective-permute-start.3) | collective-permute-done | bytes 663584 | tf_op jit(solution)/shard_map/ppermute | solution.py:17
  60.1 0.1 bitcast_add_fusion.3
  60.3 1.6 %collective-permute-start.4 = (bf16[2,648,128]{2,1,0:T(8,128)(2,1)S(1)}, bf16[2,648,128]{2,1,0:T(8,128)(2,1)S(1)}, u32[]{:S(2)}, u32[]{:S(2)}) collective-permute-start(bf16[2,648,128]{2,1,0:T(8,128)(2,1)S(1)} %fusion.16), channel_id=1, source_target_pairs={{0,16},{1,17},{2,18},{3,19},{4,20},{5,21},{6,22},{7,23},{8,24},{9,... | collective-permute-start | bytes 995336 | tf_op jit(solution)/shard_map/ppermute | solution.py:17
  61.9 0.4 collective-permute-done.5
  62.3 0.1 bitcast_add_fusion.5
  62.5 1.7 %collective-permute-start.6 = (bf16[2,648,128]{2,1,0:T(8,128)(2,1)S(1)}, bf16[2,648,128]{2,1,0:T(8,128)(2,1)S(1)}, u32[]{:S(2)}, u32[]{:S(2)}) collective-permute-start(bf16[2,648,128]{2,1,0:T(8,128)(2,1)S(1)} %fusion.17), channel_id=1, source_target_pairs={{0,1},{1,0},{2,3},{3,2},{4,5},{5,4},{6,7},{7,6},{8,9},{9,8},{10,11... | collective-permute-start | bytes 995336 | tf_op jit(solution)/shard_map/ppermute | solution.py:17
  64.2 10.1 %collective-permute-done.11 = bf16[2,2,648,128]{3,2,1,0:T(8,128)(2,1)S(1)} collective-permute-done((bf16[2,2,648,128]{3,2,1,0:T(8,128)(2,1)S(1)}, bf16[2,2,648,128]{3,2,1,0:T(8,128)(2,1)S(1)}, u32[]{:S(2)}, u32[]{:S(2)}) %collective-permute-start.11) | collective-permute-done | bytes 663584 | tf_op jit(solution)/shard_map/ppermute | solution.py:17
  74.3 0.1 bitcast_add_fusion.2
  74.5 1.6 %collective-permute-start.12 = (bf16[2,648,128]{2,1,0:T(8,128)(2,1)S(1)}, bf16[2,648,128]{2,1,0:T(8,128)(2,1)S(1)}, u32[]{:S(2)}, u32[]{:S(2)}) collective-permute-start(bf16[2,648,128]{2,1,0:T(8,128)(2,1)S(1)} %fusion.18), channel_id=1, source_target_pairs={{0,16},{1,17},{2,18},{3,19},{4,20},{5,21},{6,22},{7,23},{8,24},{9,... | collective-permute-start | bytes 995336 | tf_op jit(solution)/shard_map/ppermute | solution.py:17
  76.1 0.4 collective-permute-done.13
  76.5 0.1 bitcast_add_fusion.4
  76.7 1.7 %collective-permute-start.14 = (bf16[2,648,128]{2,1,0:T(8,128)(2,1)S(1)}, bf16[2,648,128]{2,1,0:T(8,128)(2,1)S(1)}, u32[]{:S(2)}, u32[]{:S(2)}) collective-permute-start(bf16[2,648,128]{2,1,0:T(8,128)(2,1)S(1)} %fusion.19), channel_id=1, source_target_pairs={{0,1},{1,0},{2,3},{3,2},{4,5},{5,4},{6,7},{7,6},{8,9},{9,8},{10,11... | collective-permute-start | bytes 995336 | tf_op jit(solution)/shard_map/ppermute | solution.py:17
  78.4 5.2 %collective-permute-done.4 = bf16[2,648,128]{2,1,0:T(8,128)(2,1)S(1)} collective-permute-done((bf16[2,648,128]{2,1,0:T(8,128)(2,1)S(1)}, bf16[2,648,128]{2,1,0:T(8,128)(2,1)S(1)}, u32[]{:S(2)}, u32[]{:S(2)}) %collective-permute-start.4) | collective-permute-done | bytes 331808 | tf_op jit(solution)/shard_map/ppermute | solution.py:17
  84.0 1.6 %collective-permute-start.7 = (bf16[648,128]{1,0:T(8,128)(2,1)S(1)}, bf16[648,128]{1,0:T(8,128)(2,1)S(1)}, u32[]{:S(2)}, u32[]{:S(2)}) collective-permute-start(bf16[648,128]{1,0:T(8,128)(2,1)S(1)} %get-tuple-element.11), channel_id=1, source_target_pairs={{0,2},{1,3},{2,0},{3,1},{4,6},{5,7},{6,4},{7,5},{8,10},{9,11},{10,... | collective-permute-start | bytes 497672 | tf_op jit(solution)/shard_map/ppermute | solution.py:17
  85.6 1.1 collective-permute-start.8
  86.7 1.7 %collective-permute-start.9 = (bf16[648,128]{1,0:T(8,128)(2,1)S(1)}, bf16[648,128]{1,0:T(8,128)(2,1)S(1)}, u32[]{:S(2)}, u32[]{:S(2)}) collective-permute-start(bf16[648,128]{1,0:T(8,128)(2,1)S(1)} %get-tuple-element.12), channel_id=1, source_target_pairs={{0,6},{1,7},{2,4},{3,5},{4,2},{5,3},{6,0},{7,1},{8,14},{9,15},{10,... | collective-permute-start | bytes 497672 | tf_op jit(solution)/shard_map/ppermute | solution.py:17
  88.4 1.6 %collective-permute-done.12 = bf16[2,648,128]{2,1,0:T(8,128)(2,1)S(1)} collective-permute-done((bf16[2,648,128]{2,1,0:T(8,128)(2,1)S(1)}, bf16[2,648,128]{2,1,0:T(8,128)(2,1)S(1)}, u32[]{:S(2)}, u32[]{:S(2)}) %collective-permute-start.12) | collective-permute-done | bytes 331808 | tf_op jit(solution)/shard_map/ppermute | solution.py:17
  90.3 1.6 %collective-permute-start.15 = (bf16[648,128]{1,0:T(8,128)(2,1)S(1)}, bf16[648,128]{1,0:T(8,128)(2,1)S(1)}, u32[]{:S(2)}, u32[]{:S(2)}) collective-permute-start(bf16[648,128]{1,0:T(8,128)(2,1)S(1)} %get-tuple-element.14), channel_id=1, source_target_pairs={{0,2},{1,3},{2,0},{3,1},{4,6},{5,7},{6,4},{7,5},{8,10},{9,11},{10,... | collective-permute-start | bytes 497672 | tf_op jit(solution)/shard_map/ppermute | solution.py:17
  92.0 1.1 collective-permute-start.16
  93.1 1.7 %collective-permute-start.17 = (bf16[648,128]{1,0:T(8,128)(2,1)S(1)}, bf16[648,128]{1,0:T(8,128)(2,1)S(1)}, u32[]{:S(2)}, u32[]{:S(2)}) collective-permute-start(bf16[648,128]{1,0:T(8,128)(2,1)S(1)} %get-tuple-element.15), channel_id=1, source_target_pairs={{0,6},{1,7},{2,4},{3,5},{4,2},{5,3},{6,0},{7,1},{8,14},{9,15},{10,... | collective-permute-start | bytes 497672 | tf_op jit(solution)/shard_map/ppermute | solution.py:17
  94.8 5.9 %collective-permute-done.8 = bf16[648,128]{1,0:T(8,128)(2,1)S(1)} collective-permute-done((bf16[648,128]{1,0:T(8,128)(2,1)S(1)}, bf16[648,128]{1,0:T(8,128)(2,1)S(1)}, u32[]{:S(2)}, u32[]{:S(2)}) %collective-permute-start.8) | collective-permute-done | bytes 165920 | tf_op jit(solution)/shard_map/ppermute | solution.py:17
  100.8 0.1 collective-permute-done.15
  100.9 13.2 %collective-permute-done.16 = bf16[648,128]{1,0:T(8,128)(2,1)S(1)} collective-permute-done((bf16[648,128]{1,0:T(8,128)(2,1)S(1)}, bf16[648,128]{1,0:T(8,128)(2,1)S(1)}, u32[]{:S(2)}, u32[]{:S(2)}) %collective-permute-start.16) | collective-permute-done | bytes 165920 | tf_op jit(solution)/shard_map/ppermute | solution.py:17
  114.1 0.7 copy-done.7
  114.8 0.7 copy-done.8
  115.5 1.5 fusion.8
  117.1 1.2 collective-permute-done.18
  118.4 0.6 collective-permute-start.19
  118.9 3.7 %collective-permute-done.19 = f32[128,128]{1,0:T(8,128)S(1)} collective-permute-done((f32[128,128]{1,0:T(8,128)S(1)}, f32[128,128]{1,0:T(8,128)S(1)}, u32[]{:S(2)}, u32[]{:S(2)}) %collective-permute-start.19) | collective-permute-done | bytes 65568 | tf_op jit(solution)/shard_map/ppermute | solution.py:17
  122.7 1.7 %collective-permute-start.20 = (f32[128,128]{1,0:T(8,128)S(1)}, f32[128,128]{1,0:T(8,128)S(1)}, u32[]{:S(2)}, u32[]{:S(2)}) collective-permute-start(f32[128,128]{1,0:T(8,128)S(1)} %add.166), channel_id=1, source_target_pairs={{0,2},{1,3},{2,0},{3,1},{4,6},{5,7},{6,4},{7,5},{8,10},{9,11},{10,... | collective-permute-start | bytes 196616 | tf_op jit(solution)/shard_map/ppermute | solution.py:17
  124.4 2.6 %collective-permute-done.20 = f32[128,128]{1,0:T(8,128)S(1)} collective-permute-done((f32[128,128]{1,0:T(8,128)S(1)}, f32[128,128]{1,0:T(8,128)S(1)}, u32[]{:S(2)}, u32[]{:S(2)}) %collective-permute-start.20) | collective-permute-done | bytes 65568 | tf_op jit(solution)/shard_map/ppermute | solution.py:17
  127.1 2.7 %collective-permute-start.21 = (f32[128,128]{1,0:T(8,128)S(1)}, f32[128,128]{1,0:T(8,128)S(1)}, u32[]{:S(2)}, u32[]{:S(2)}) collective-permute-start(f32[128,128]{1,0:T(8,128)S(1)} %add.167), channel_id=1, source_target_pairs={{0,4},{1,5},{2,6},{3,7},{4,0},{5,1},{6,2},{7,3},{8,12},{9,13},{10,... | collective-permute-start | bytes 196616 | tf_op jit(solution)/shard_map/ppermute | solution.py:17
  129.8 2.5 %collective-permute-done.21 = f32[128,128]{1,0:T(8,128)S(1)} collective-permute-done((f32[128,128]{1,0:T(8,128)S(1)}, f32[128,128]{1,0:T(8,128)S(1)}, u32[]{:S(2)}, u32[]{:S(2)}) %collective-permute-start.21) | collective-permute-done | bytes 65568 | tf_op jit(solution)/shard_map/ppermute | solution.py:17
  132.3 1.6 %collective-permute-start.22 = (f32[128,128]{1,0:T(8,128)S(1)}, f32[128,128]{1,0:T(8,128)S(1)}, u32[]{:S(2)}, u32[]{:S(2)}) collective-permute-start(f32[128,128]{1,0:T(8,128)S(1)} %add.168), channel_id=1, source_target_pairs={{0,16},{1,17},{2,18},{3,19},{4,20},{5,21},{6,22},{7,23},{8,24},{9,... | collective-permute-start | bytes 196616 | tf_op jit(solution)/shard_map/ppermute | solution.py:17
  133.9 2.7 %collective-permute-done.22 = f32[128,128]{1,0:T(8,128)S(1)} collective-permute-done((f32[128,128]{1,0:T(8,128)S(1)}, f32[128,128]{1,0:T(8,128)S(1)}, u32[]{:S(2)}, u32[]{:S(2)}) %collective-permute-start.22) | collective-permute-done | bytes 65568 | tf_op jit(solution)/shard_map/ppermute | solution.py:17
  136.6 0.6 add.169.gram_ref
  137.3 9.4 %inverse.1 = f32[128,128]{1,0:T(8,128)} custom-call(f32[128,128]{1,0:T(8,128)} %add.169.gram_ref), custom_call_target="tpu_custom_call" | custom-call | tf_op jit(solution)/shard_map/inverse/pallas_call | solution.py:109
  146.7 1.5 collective-permute-done.23
  148.2 1.7 %fusion.3 = f32[1,648,128]{2,1,0:T(8,128)S(1)} fusion(f32[128,128]{1,0:T(8,128)} %inverse.1, f32[128,128]{1,0:T(8,128)S(1)} %collective-permute-done.23, pred[]{:T(512)S(6)} %eq.6, bf16[648,128]{1,0:T(8,128)(2,1)S(1)} %collective-permute-done.9, bf16[648,128]{1,0:T(8,128)(2,1)S(1)} %collective-permute-done.8, ...), kind=kOutput, calls=%fused_computation.20 | convolution fusion | flops 127998976 | bytes 1292293 | tf_op jit(solution)/shard_map/dot_general | solution.py:182
  149.8 1.9 %fusion.2 = f32[1,648,128]{2,1,0:T(8,128)S(1)} fusion(f32[128,128]{1,0:T(8,128)} %inverse.1, f32[128,128]{1,0:T(8,128)S(1)} %collective-permute-done.23, pred[]{:T(512)S(6)} %eq.7, bf16[648,128]{1,0:T(8,128)(2,1)} %copy-done.8, bf16[648,128]{1,0:T(8,128)(2,1)} %copy-done.7, bf16[648,128]{1,0:T(8,128)(2,1)} %copy-done.6, f32[4,648,128]{2,1,0:T(8,128)} %bitcast.130, ...), kind=kOutput, calls=%fused_computation.18 | convolution fusion | flops 127998976 | bytes 1292293 | tf_op jit(solution)/shard_map/dot_general | solution.py:182
  151.8 0.9 pad_maximum_fusion.2
  (55 shorter events, 1.5 us)
Async XLA Ops:
  0.0 1.4 copy-start
  1.4 7.8 %copy-start.5 = (bf16[2,1,8,2,32,768]{5,4,3,2,1,0:T(8,128)(2,1)S(1)}, bf16[2,1,8,2,32,768]{5,4,3,2,1,0:T(8,128)(2,1)}, u32[]{:S(2)}) copy-start(bf16[2,1,8,2,32,768]{5,4,3,2,1,0:T(8,128)(2,1)} %param.3) | copy-start | bytes 4718596
  3.1 7.6 %collective-permute-start = (bf16[2,8,1,32,128]{4,3,2,1,0:T(8,128)(2,1)S(1)}, bf16[2,8,1,32,128]{4,3,2,1,0:T(8,128)(2,1)S(1)}, u32[]{:S(2)}, u32[]{:S(2)}) collective-permute-start(bf16[2,8,1,32,128]{4,3,2,1,0:T(8,128)(2,1)S(1)} %get-tuple-element.19), channel_id=1, source_target_pairs={{0,1},{1,2},{2,3},{3,4},{4,5},{5,6},{6,7},{8,9},{9,10},{10,11},{11... | collective-permute-start | bytes 393224 | tf_op jit(solution)/shard_map/ppermute | solution.py:23
  7.9 6.9 %collective-permute-start.1 = (bf16[2,8,1,32,128]{4,3,2,1,0:T(8,128)(2,1)S(1)}, bf16[2,8,1,32,128]{4,3,2,1,0:T(8,128)(2,1)S(1)}, u32[]{:S(2)}, u32[]{:S(2)}) collective-permute-start(bf16[2,8,1,32,128]{4,3,2,1,0:T(8,128)(2,1)S(1)} %get-tuple-element.20), channel_id=1, source_target_pairs={{1,0},{2,1},{3,2},{4,3},{5,4},{6,5},{7,6},{9,8},{10,9},{11,10},{12... | collective-permute-start | bytes 393224 | tf_op jit(solution)/shard_map/ppermute | solution.py:24
  20.8 4.7 %copy-start.3 = (f32[27,768,128]{2,1,0:T(8,128)}, f32[27,768,128]{2,1,0:T(8,128)S(1)}, u32[]{:S(2)}) copy-start(f32[27,768,128]{2,1,0:T(8,128)S(1)} %product.2) | copy-start | bytes 31850500
  22.9 14.5 %collective-permute-start.2 = (bf16[2,2,2,2,648,128]{5,4,3,2,1,0:T(8,128)(2,1)}, bf16[2,2,2,2,648,128]{5,4,3,2,1,0:T(8,128)(2,1)}, u32[]{:S(2)}, u32[]{:S(2)}) collective-permute-start(bf16[2,2,2,2,648,128]{5,4,3,2,1,0:T(8,128)(2,1)} %fusion), channel_id=1, source_target_pairs={{0,8},{1,9},{2,10},{3,11},{4,12},{5,13},{6,14},{7,15},{8,0},{9,1},... | collective-permute-start | bytes 7962632 | tf_op jit(solution)/shard_map/ppermute | solution.py:17
  31.5 4.1 %copy-start.2 = (f32[27,768,128]{2,1,0:T(8,128)}, f32[27,768,128]{2,1,0:T(8,128)S(1)}, u32[]{:S(2)}) copy-start(f32[27,768,128]{2,1,0:T(8,128)S(1)} %product.3) | copy-start | bytes 31850500
  37.5 8.6 %collective-permute-start.10 = (bf16[2,2,2,2,648,128]{5,4,3,2,1,0:T(8,128)(2,1)}, bf16[2,2,2,2,648,128]{5,4,3,2,1,0:T(8,128)(2,1)}, u32[]{:S(2)}, u32[]{:S(2)}) collective-permute-start(bf16[2,2,2,2,648,128]{5,4,3,2,1,0:T(8,128)(2,1)} %fusion.1), channel_id=1, source_target_pairs={{0,8},{1,9},{2,10},{3,11},{4,12},{5,13},{6,14},{7,15},{8,0},{9,1},... | collective-permute-start | bytes 7962632 | tf_op jit(solution)/shard_map/ppermute | solution.py:17
  37.5 8.6 %slice-start = ((s8[10616832]{0:T(1024)(128)(4,1)}), s8[4194304]{0:T(1024)(128)(4,1)S(1)}, s32[]{:S(2)}) async-start(s8[10616832]{0:T(1024)(128)(4,1)} %bitcast.118), calls=%async_computation | async-start | bytes 8388608
  37.5 8.6 %slice-start.1 = ((s8[10616832]{0:T(1024)(128)(4,1)}), s8[4194304]{0:T(1024)(128)(4,1)S(1)}, s32[]{:S(2)}) async-start(s8[10616832]{0:T(1024)(128)(4,1)} %bitcast.118), calls=%async_computation.1 | async-start | bytes 8388608
  41.4 4.7 %slice-start.2 = ((s8[10616832]{0:T(1024)(128)(4,1)}), s8[2228224]{0:T(1024)(128)(4,1)S(1)}, s32[]{:S(2)}) async-start(s8[10616832]{0:T(1024)(128)(4,1)} %bitcast.118), calls=%async_computation.2 | async-start | bytes 4456448
  41.8 18.3 %collective-permute-start.3 = (bf16[2,2,648,128]{3,2,1,0:T(8,128)(2,1)S(1)}, bf16[2,2,648,128]{3,2,1,0:T(8,128)(2,1)S(1)}, u32[]{:S(2)}, u32[]{:S(2)}) collective-permute-start(bf16[2,2,648,128]{3,2,1,0:T(8,128)(2,1)S(1)} %fusion.6), channel_id=1, source_target_pairs={{0,1},{1,0},{2,3},{3,2},{4,5},{5,4},{6,7},{7,6},{8,9},{9,8},{10,11... | collective-permute-start | bytes 1990664 | tf_op jit(solution)/shard_map/ppermute | solution.py:17
  44.5 17.8 %collective-permute-start.5 = (bf16[2,2,648,128]{3,2,1,0:T(8,128)(2,1)S(1)}, bf16[2,2,648,128]{3,2,1,0:T(8,128)(2,1)S(1)}, u32[]{:S(2)}, u32[]{:S(2)}) collective-permute-start(bf16[2,2,648,128]{3,2,1,0:T(8,128)(2,1)S(1)} %fusion.4), channel_id=1, source_target_pairs={{0,16},{1,17},{2,18},{3,19},{4,20},{5,21},{6,22},{7,23},{8,24},{9,... | collective-permute-start | bytes 1990664 | tf_op jit(solution)/shard_map/ppermute | solution.py:17
  48.8 25.5 %collective-permute-start.11 = (bf16[2,2,648,128]{3,2,1,0:T(8,128)(2,1)S(1)}, bf16[2,2,648,128]{3,2,1,0:T(8,128)(2,1)S(1)}, u32[]{:S(2)}, u32[]{:S(2)}) collective-permute-start(bf16[2,2,648,128]{3,2,1,0:T(8,128)(2,1)S(1)} %fusion.7), channel_id=1, source_target_pairs={{0,1},{1,0},{2,3},{3,2},{4,5},{5,4},{6,7},{7,6},{8,9},{9,8},{10,11... | collective-permute-start | bytes 1990664 | tf_op jit(solution)/shard_map/ppermute | solution.py:17
  49.5 27.1 %collective-permute-start.13 = (bf16[2,2,648,128]{3,2,1,0:T(8,128)(2,1)S(1)}, bf16[2,2,648,128]{3,2,1,0:T(8,128)(2,1)S(1)}, u32[]{:S(2)}, u32[]{:S(2)}) collective-permute-start(bf16[2,2,648,128]{3,2,1,0:T(8,128)(2,1)S(1)} %fusion.5), channel_id=1, source_target_pairs={{0,16},{1,17},{2,18},{3,19},{4,20},{5,21},{6,22},{7,23},{8,24},{9,... | collective-permute-start | bytes 1990664 | tf_op jit(solution)/shard_map/ppermute | solution.py:17
  60.3 23.3 %collective-permute-start.4 = (bf16[2,648,128]{2,1,0:T(8,128)(2,1)S(1)}, bf16[2,648,128]{2,1,0:T(8,128)(2,1)S(1)}, u32[]{:S(2)}, u32[]{:S(2)}) collective-permute-start(bf16[2,648,128]{2,1,0:T(8,128)(2,1)S(1)} %fusion.16), channel_id=1, source_target_pairs={{0,16},{1,17},{2,18},{3,19},{4,20},{5,21},{6,22},{7,23},{8,24},{9,... | collective-permute-start | bytes 995336 | tf_op jit(solution)/shard_map/ppermute | solution.py:17
  62.5 21.2 %collective-permute-start.6 = (bf16[2,648,128]{2,1,0:T(8,128)(2,1)S(1)}, bf16[2,648,128]{2,1,0:T(8,128)(2,1)S(1)}, u32[]{:S(2)}, u32[]{:S(2)}) collective-permute-start(bf16[2,648,128]{2,1,0:T(8,128)(2,1)S(1)} %fusion.17), channel_id=1, source_target_pairs={{0,1},{1,0},{2,3},{3,2},{4,5},{5,4},{6,7},{7,6},{8,9},{9,8},{10,11... | collective-permute-start | bytes 995336 | tf_op jit(solution)/shard_map/ppermute | solution.py:17
  74.5 15.5 %collective-permute-start.12 = (bf16[2,648,128]{2,1,0:T(8,128)(2,1)S(1)}, bf16[2,648,128]{2,1,0:T(8,128)(2,1)S(1)}, u32[]{:S(2)}, u32[]{:S(2)}) collective-permute-start(bf16[2,648,128]{2,1,0:T(8,128)(2,1)S(1)} %fusion.18), channel_id=1, source_target_pairs={{0,16},{1,17},{2,18},{3,19},{4,20},{5,21},{6,22},{7,23},{8,24},{9,... | collective-permute-start | bytes 995336 | tf_op jit(solution)/shard_map/ppermute | solution.py:17
  76.7 13.4 %collective-permute-start.14 = (bf16[2,648,128]{2,1,0:T(8,128)(2,1)S(1)}, bf16[2,648,128]{2,1,0:T(8,128)(2,1)S(1)}, u32[]{:S(2)}, u32[]{:S(2)}) collective-permute-start(bf16[2,648,128]{2,1,0:T(8,128)(2,1)S(1)} %fusion.19), channel_id=1, source_target_pairs={{0,1},{1,0},{2,3},{3,2},{4,5},{5,4},{6,7},{7,6},{8,9},{9,8},{10,11... | collective-permute-start | bytes 995336 | tf_op jit(solution)/shard_map/ppermute | solution.py:17
  84.0 9.1 %collective-permute-start.7 = (bf16[648,128]{1,0:T(8,128)(2,1)S(1)}, bf16[648,128]{1,0:T(8,128)(2,1)S(1)}, u32[]{:S(2)}, u32[]{:S(2)}) collective-permute-start(bf16[648,128]{1,0:T(8,128)(2,1)S(1)} %get-tuple-element.11), channel_id=1, source_target_pairs={{0,2},{1,3},{2,0},{3,1},{4,6},{5,7},{6,4},{7,5},{8,10},{9,11},{10,... | collective-permute-start | bytes 497672 | tf_op jit(solution)/shard_map/ppermute | solution.py:17
  85.6 15.1 %collective-permute-start.8 = (bf16[648,128]{1,0:T(8,128)(2,1)S(1)}, bf16[648,128]{1,0:T(8,128)(2,1)S(1)}, u32[]{:S(2)}, u32[]{:S(2)}) collective-permute-start(bf16[648,128]{1,0:T(8,128)(2,1)S(1)} %get-tuple-element.13), channel_id=1, source_target_pairs={{0,4},{1,5},{2,6},{3,7},{4,0},{5,1},{6,2},{7,3},{8,12},{9,13},{10,... | collective-permute-start | bytes 497672 | tf_op jit(solution)/shard_map/ppermute | solution.py:17
  86.7 14.0 %collective-permute-start.9 = (bf16[648,128]{1,0:T(8,128)(2,1)S(1)}, bf16[648,128]{1,0:T(8,128)(2,1)S(1)}, u32[]{:S(2)}, u32[]{:S(2)}) collective-permute-start(bf16[648,128]{1,0:T(8,128)(2,1)S(1)} %get-tuple-element.12), channel_id=1, source_target_pairs={{0,6},{1,7},{2,4},{3,5},{4,2},{5,3},{6,0},{7,1},{8,14},{9,15},{10,... | collective-permute-start | bytes 497672 | tf_op jit(solution)/shard_map/ppermute | solution.py:17
  90.2 25.3 %copy-start.4 = (f32[2,2,648,128]{3,2,1,0:T(8,128)}, f32[2,2,648,128]{3,2,1,0:T(8,128)S(1)}, u32[]{:S(2)}) copy-start(f32[2,2,648,128]{3,2,1,0:T(8,128)S(1)} %pad_maximum_fusion.1) | copy-start | bytes 3981316
  90.3 10.6 %collective-permute-start.15 = (bf16[648,128]{1,0:T(8,128)(2,1)S(1)}, bf16[648,128]{1,0:T(8,128)(2,1)S(1)}, u32[]{:S(2)}, u32[]{:S(2)}) collective-permute-start(bf16[648,128]{1,0:T(8,128)(2,1)S(1)} %get-tuple-element.14), channel_id=1, source_target_pairs={{0,2},{1,3},{2,0},{3,1},{4,6},{5,7},{6,4},{7,5},{8,10},{9,11},{10,... | collective-permute-start | bytes 497672 | tf_op jit(solution)/shard_map/ppermute | solution.py:17
  92.0 22.1 %collective-permute-start.16 = (bf16[648,128]{1,0:T(8,128)(2,1)S(1)}, bf16[648,128]{1,0:T(8,128)(2,1)S(1)}, u32[]{:S(2)}, u32[]{:S(2)}) collective-permute-start(bf16[648,128]{1,0:T(8,128)(2,1)S(1)} %get-tuple-element.16), channel_id=1, source_target_pairs={{0,4},{1,5},{2,6},{3,7},{4,0},{5,1},{6,2},{7,3},{8,12},{9,13},{10,... | collective-permute-start | bytes 497672 | tf_op jit(solution)/shard_map/ppermute | solution.py:17
  93.1 21.0 %collective-permute-start.17 = (bf16[648,128]{1,0:T(8,128)(2,1)S(1)}, bf16[648,128]{1,0:T(8,128)(2,1)S(1)}, u32[]{:S(2)}, u32[]{:S(2)}) collective-permute-start(bf16[648,128]{1,0:T(8,128)(2,1)S(1)} %get-tuple-element.15), channel_id=1, source_target_pairs={{0,6},{1,7},{2,4},{3,5},{4,2},{5,3},{6,0},{7,1},{8,14},{9,15},{10,... | collective-permute-start | bytes 497672 | tf_op jit(solution)/shard_map/ppermute | solution.py:17
  100.9 45.8 %copy-start.6 = (bf16[648,128]{1,0:T(8,128)(2,1)}, bf16[648,128]{1,0:T(8,128)(2,1)S(1)}, u32[]{:S(2)}) copy-start(bf16[648,128]{1,0:T(8,128)(2,1)S(1)} %collective-permute-done.15) | copy-start | bytes 497668
  114.1 0.7 copy-start.7
  114.8 0.7 copy-start.8
  117.0 1.3 collective-permute-start.18
  118.4 4.3 %collective-permute-start.19 = (f32[128,128]{1,0:T(8,128)S(1)}, f32[128,128]{1,0:T(8,128)S(1)}, u32[]{:S(2)}, u32[]{:S(2)}) collective-permute-start(f32[128,128]{1,0:T(8,128)S(1)} %bitcast_add_fusion.12), channel_id=1, source_target_pairs={{0,1},{1,0},{2,3},{3,2},{4,5},{5,4},{6,7},{7,6},{8,9},{9,8},{10,11... | collective-permute-start | bytes 196616 | tf_op jit(solution)/shard_map/ppermute | solution.py:17
  122.7 4.3 %collective-permute-start.20 = (f32[128,128]{1,0:T(8,128)S(1)}, f32[128,128]{1,0:T(8,128)S(1)}, u32[]{:S(2)}, u32[]{:S(2)}) collective-permute-start(f32[128,128]{1,0:T(8,128)S(1)} %add.166), channel_id=1, source_target_pairs={{0,2},{1,3},{2,0},{3,1},{4,6},{5,7},{6,4},{7,5},{8,10},{9,11},{10,... | collective-permute-start | bytes 196616 | tf_op jit(solution)/shard_map/ppermute | solution.py:17
  127.1 5.2 %collective-permute-start.21 = (f32[128,128]{1,0:T(8,128)S(1)}, f32[128,128]{1,0:T(8,128)S(1)}, u32[]{:S(2)}, u32[]{:S(2)}) collective-permute-start(f32[128,128]{1,0:T(8,128)S(1)} %add.167), channel_id=1, source_target_pairs={{0,4},{1,5},{2,6},{3,7},{4,0},{5,1},{6,2},{7,3},{8,12},{9,13},{10,... | collective-permute-start | bytes 196616 | tf_op jit(solution)/shard_map/ppermute | solution.py:17
  132.3 4.3 %collective-permute-start.22 = (f32[128,128]{1,0:T(8,128)S(1)}, f32[128,128]{1,0:T(8,128)S(1)}, u32[]{:S(2)}, u32[]{:S(2)}) collective-permute-start(f32[128,128]{1,0:T(8,128)S(1)} %add.168), channel_id=1, source_target_pairs={{0,16},{1,17},{2,18},{3,19},{4,20},{5,21},{6,22},{7,23},{8,24},{9,... | collective-permute-start | bytes 196616 | tf_op jit(solution)/shard_map/ppermute | solution.py:17
  146.7 1.5 collective-permute-start.23
  148.2 4.5 %copy-start.1 = (bf16[2,1,8,2,32,768]{5,4,3,2,1,0:T(8,128)(2,1)S(1)}, bf16[2,1,8,2,32,768]{5,4,3,2,1,0:T(8,128)(2,1)}, u32[]{:S(2)}) copy-start(bf16[2,1,8,2,32,768]{5,4,3,2,1,0:T(8,128)(2,1)} %param.4) | copy-start | bytes 4718596

commit v2 on v1

--- a/solution.py
+++ b/solution.py
@@ -3,6 +3,7 @@
 
 import jax
 import jax.numpy as jnp
+import numpy as np
 from jax import lax
 from jax.experimental import pallas as pl
 from jax.experimental.pallas import tpu as pltpu
@@ -183,9 +184,250 @@
     return jnp.stack(basis)
 
 
+DP_BITS, SPACE_BITS = 2, 3
+UNITS = 28
+
+
+@functools.lru_cache
+def unit_tables():
+    table = np.zeros((32, 4 * UNITS + 32 + 27), np.int32)
+    for device in range(32):
+        y, core, z, x = device >> 4, (device >> 3) & 1, (device >> 1) & 3, device & 1
+        quarter = 2 * y + x
+        first = 16 * core + 4 * quarter
+        def units_for(target):
+            return [4 * k + s for k in range(27) for s in range(4) if ((32 * k + first + s) // 54) % 4 == target]
+        row = []
+        for m in range(4):
+            units = units_for(z ^ m)
+            row += units + [108] * (UNITS - len(units))
+        held = units_for(z)
+        for m in range(4):
+            for other in range(2):
+                q = quarter ^ m
+                target = ((q >> 1) << 4) | ((core ^ other) << 3) | (z << 1) | (q & 1)
+                for s in range(4):
+                    found = [p for p, n in enumerate(held) if n % 4 == s and (8 * (n - s) + first + s) // 27 == target]
+                    row.append(found[0] if found else UNITS)
+        for v in range(27):
+            column = (27 * device + v) % 32
+            row.append(16 * ((column // 16) ^ core) + 4 * (((column % 16) // 4) ^ quarter) + column % 4)
+        table[device] = row
+    return table
+
+
+def turn_kernel(frames, chunk, half, where_ref, own_ref, got_ref, out_ref):
+    at = pl.multiple_of(where_ref[0] * half, 128)
+    for t in range(frames):
+        rows = slice(chunk * t, chunk * (t + 1))
+        block = jnp.concatenate([own_ref[rows, pl.ds(at, half)], got_ref[rows, :]], axis=0)
+        out_ref[:, :, 2 * chunk * t : 2 * chunk * (t + 1)] = block.T.reshape(4, half // 4, 2 * chunk)
+
+
+def turn(where, own, got, frames):
+    positions, half = got.shape
+    return pl.pallas_call(
+        functools.partial(turn_kernel, frames, positions // frames, half),
+        in_specs=[pl.BlockSpec(memory_space=pltpu.SMEM)] + [pl.BlockSpec(memory_space=pltpu.VMEM)] * 2,
+        out_specs=pl.BlockSpec(memory_space=pltpu.VMEM),
+        out_shape=jax.ShapeDtypeStruct((4, half // 4, 2 * positions), BF16),
+        cost_estimate=pl.CostEstimate(flops=0, bytes_accessed=8 * positions * half, transcendentals=0),
+        name="turn",
+    )(where, own, got)
+
+
+def plane_kernel(frames, widths, rank, where_ref, table_ref, act_ref, a1, a2, a3, own_ref, other_ref,
+                 keep_ref, s1, s2, s3, lhs, wide, acc, units):
+    x, quarter = where_ref[1], where_ref[2]
+    each = act_ref.shape[1]
+    depth = act_ref.shape[2]
+    frame = depth // frames
+    for m, ref in enumerate((act_ref, a1, a2, a3)):
+        value = ref[quarter] if m == 0 else ref[...]
+        zero = jnp.zeros((each, frame), BF16)
+        lhs[m, 0:each, 0:frame] = zero
+        lhs[m, 0:each, frame:] = value[:, : depth - frame]
+        lhs[m, each : 2 * each, :] = value
+        lhs[m, 2 * each :, : depth - frame] = value[:, frame:]
+        lhs[m, 2 * each :, depth - frame :] = zero
+    rows = frames * 3 * widths
+    at = lax.rem(lax.broadcasted_iota(jnp.int32, (rows, rank), 0), widths)
+    for side, ref in enumerate((own_ref, other_ref)):
+        for m in range(4):
+            piece = ref[m]
+            to = pl.ds(3 * (x ^ (m & 1)), 3)
+            flat = piece.astype(F32).reshape(rows, rank)
+            later = jnp.where(at == widths - 1, 0.0, pltpu.roll(flat, rows - 1, 0))
+            earlier = jnp.where(at == 0, 0.0, pltpu.roll(flat, 1, 0))
+            wide[m >> 1, :, side, to, :, 0:rank] = later.astype(BF16).reshape(piece.shape)
+            wide[m >> 1, :, side, to, :, rank : 2 * rank] = piece
+            wide[m >> 1, :, side, to, :, 2 * rank :] = earlier.astype(BF16).reshape(piece.shape)
+
+    blocks = each // 24
+    units[27 * blocks] = jnp.zeros((24, rank), F32)
+
+    @pl.loop(0, 3)
+    def _(along_h):
+        for m in range(4):
+            window = wide[m >> 1, :, :, pl.ds(2 * (x ^ (m & 1)) + 2 - along_h, 2)]
+            made = jnp.dot(lhs[m], window.reshape(depth, 3 * rank), preferred_element_type=F32)
+            acc[...] = made if m == 0 else acc[...] + made
+        for a in range(3):
+            for c in range(3):
+                part = acc[a * each : (a + 1) * each, c * rank : (c + 1) * rank]
+                units[pl.ds((9 * a + 3 * along_h + c) * blocks, blocks)] = part.reshape(blocks, 24, rank)
+
+    @pl.loop(0, UNITS)
+    def _(p):
+        keep_ref[p] = units[table_ref[p]]
+        for m, ref in enumerate((s1, s2, s3)):
+            ref[p] = units[table_ref[(m + 1) * UNITS + p]].astype(BF16)
+
+
+def plane(where, table, act, got, own, other):
+    frames, _, widths, rank = own.shape[1:]
+    each, depth = act.shape[1:]
+    vmem = pl.BlockSpec(memory_space=pltpu.VMEM)
+    smem = pl.BlockSpec(memory_space=pltpu.SMEM)
+    return pl.pallas_call(
+        functools.partial(plane_kernel, frames, widths, rank),
+        in_specs=[smem, smem] + [vmem] * 6,
+        out_specs=[vmem] * 4,
+        out_shape=[jax.ShapeDtypeStruct((UNITS, 24, rank), F32)]
+        + [jax.ShapeDtypeStruct((UNITS, 24, rank), BF16)] * 3,
+        scratch_shapes=[
+            pltpu.VMEM((4, 3 * each, depth), BF16),
+            pltpu.VMEM((2, frames, 2, 6, widths, 3 * rank), BF16),
+            pltpu.VMEM((3 * each, 3 * rank), F32),
+            pltpu.VMEM((27 * each // 24 + 1, 24, rank), F32),
+        ],
+        compiler_params=pltpu.CompilerParams(vmem_limit_bytes=30 * 2**20),
+        cost_estimate=pl.CostEstimate(
+            flops=2 * 27 * 4 * depth * each * rank, bytes_accessed=6 * 2**20, transcendentals=0
+        ),
+        name="plane",
+    )(where, table, act, *got, own, other)
+
+
+def gather_kernel(rank, table_ref, keep_ref, g1, g2, g3, gram_ref, p0, p1, p2, p3, rows):
+    total = keep_ref[...] + (g1[...].astype(F32) + g2[...].astype(F32) + g3[...].astype(F32))
+    rows[0:UNITS] = total
+    rows[UNITS] = jnp.zeros((24, rank), F32)
+    for m, ref in enumerate((p0, p1, p2, p3)):
+        for other in range(2):
+            for s in range(4):
+                ref[other, s] = rows[table_ref[4 * UNITS + 8 * m + 4 * other + s]]
+    flat = total.reshape(UNITS * 24, rank)
+    gram_ref[...] = lax.dot_general(
+        flat, flat, (((0,), (0,)), ((), ())), precision=HIGHEST, preferred_element_type=F32
+    )
+
+
+def gather(table, keep, got):
+    rank = keep.shape[-1]
+    vmem = pl.BlockSpec(memory_space=pltpu.VMEM)
+    return pl.pallas_call(
+        functools.partial(gather_kernel, rank),
+        in_specs=[pl.BlockSpec(memory_space=pltpu.SMEM)] + [vmem] * 4,
+        out_specs=[vmem] * 5,
+        out_shape=[jax.ShapeDtypeStruct((rank, rank), F32)] + [jax.ShapeDtypeStruct((2, 4, 24, rank), F32)] * 4,
+        scratch_shapes=[pltpu.VMEM((UNITS + 1, 24, rank), F32)],
+        cost_estimate=pl.CostEstimate(flops=12 * UNITS * 24 * rank * rank, bytes_accessed=2**20, transcendentals=0),
+        name="gather",
+    )(table, keep, *got)
+
+
+def basis_kernel(scale, where_ref, table_ref, own0, own1, other0, other1, mine_ref, theirs_ref, out_ref, rows):
+    core = where_ref[0]
+    for layer, refs in enumerate(((own0, other0), (own1, other1))):
+        for v in range(27):
+            n = table_ref[4 * UNITS + 32 + v]
+
+            @pl.when(n < 16)
+            def _():
+                rows[24 * v : 24 * v + 24, :] = refs[0][n]
+
+            @pl.when(n >= 16)
+            def _():
+                rows[24 * v : 24 * v + 24, :] = refs[1][n - 16]
+
+        inverse = jnp.where(core == layer, mine_ref[...], theirs_ref[...])
+        made = lax.dot_general(
+            rows[...], inverse, (((1,), (1,)), ((), ())), precision=HIGHEST, preferred_element_type=F32
+        )
+        out_ref[layer] = made * scale
+
+
+def basis_of(where, table, own, other, mine, theirs, scale):
+    rank = mine.shape[0]
+    vmem = pl.BlockSpec(memory_space=pltpu.VMEM)
+    smem = pl.BlockSpec(memory_space=pltpu.SMEM)
+    return pl.pallas_call(
+        functools.partial(basis_kernel, scale),
+        in_specs=[smem, smem] + [vmem] * 6,
+        out_specs=vmem,
+        out_shape=jax.ShapeDtypeStruct((2, 27 * 24, rank), F32),
+        scratch_shapes=[pltpu.VMEM((27 * 24, rank), F32)],
+        name="basis",
+    )(where, table, *own, *other, mine, theirs)
+
+
+def planes(activations, out_grads, omega):
+    layer_count, _, frames, height, widths, channels = activations.shape
+    rank = omega.shape[1]
+    dp, space = lax.axis_index("dp"), lax.axis_index("space")
+    core, x = dp & 1, space & 1
+    quarter = 2 * (dp >> 1) + x
+    me = 8 * dp + space
+    move = functools.partial(swap, total=32)
+    core_mask, chip_masks, z_masks = 8, (1, 16, 17), (2, 4, 6)
+    where = jnp.stack([core, x, quarter]).astype(jnp.int32)
+    table = lax.dynamic_index_in_dim(jnp.asarray(unit_tables()), me, 0, keepdims=False)
+    positions, half = frames * height * widths, channels // 2
+
+    acts = [activations[layer].reshape(positions, channels) for layer in range(2)]
+    over = [lax.dynamic_slice_in_dim(a, (1 - core) * half, half, axis=1) for a in acts]
+    over = [move(a, core_mask) for a in over]
+
+    sketched = jnp.dot(out_grads.reshape(-1, channels), omega, preferred_element_type=F32).astype(BF16)
+    sketched = sketched.reshape(layer_count, frames, height, widths, rank)
+    edge = jnp.where(x == 1, sketched[:, :, height - 1], sketched[:, :, 0])
+    pairs = [(i, i + 1) for i in range(1, 7, 2)]
+    edge = lax.ppermute(edge, "space", pairs + [(j, i) for i, j in pairs])[:, :, None]
+    pieces = jnp.where(
+        x == 1, jnp.concatenate([sketched, edge], axis=2), jnp.concatenate([edge, sketched], axis=2)
+    )
+
+    grams, kept, sent = [], [], []
+    for layer in range(2):
+        act = turn(where, acts[layer], over[layer], frames)
+        got = [move(pick(act, quarter ^ (m + 1), 0), mask) for m, mask in enumerate(chip_masks)]
+        own = jnp.stack([pieces[layer]] + [move(pieces[layer], mask) for mask in chip_masks])
+        other = move(own, core_mask)
+        keep, *out = plane(where, table, act, got, own, other)
+        got = [move(value, mask) for value, mask in zip(out, z_masks)]
+        gram, *slots = gather(table, keep, got)
+        slots = [slots[0]] + [move(slots[m + 1], mask) for m, mask in enumerate(chip_masks)]
+        grams.append(gram)
+        kept.append(jnp.concatenate([s[0] for s in slots]))
+        sent.append(move(jnp.concatenate([s[1] for s in slots]), core_mask))
+
+    mine = jnp.where(core == 0, grams[0], grams[1]) + move(jnp.where(core == 0, grams[1], grams[0]), core_mask)
+    for mask in (1, 16, 2, 4):
+        mine = mine + move(mine, mask)
+    inverse = inverse_of_factor(mine)
+    theirs = move(inverse, core_mask)
+    return basis_of(where, table, kept, sent, inverse, theirs, math.sqrt(27 * channels))
+
+
 def solution(mesh):
+    def body(activations, out_grads, omega):
+        fits = (lax.axis_size("dp"), lax.axis_size("space")) == (4, 8)
+        fits = fits and activations.shape == (2, 1, 8, 2, 32, 768) and omega.shape[1] == 128
+        return (planes if fits else shards)(activations, out_grads, omega)
+
     return jax.shard_map(
-        shards,
+        body,
         mesh=mesh,
         in_specs=(
             P(None, "dp", None, "space", None, None),

time: 153 us -> 146 us (0.954)
  waiting for transfers between devices: 65.7 us -> 33.2 us
  Pallas kernels: 21.3 us -> 40 us
  starting transfers between devices: 34.5 us -> 51.4 us
  matrix products: 6.68 us -> 1.5 us
  local copies, waits for them, and re-layouts: 15 us -> 12.4 us
  other arithmetic: 9 us -> 6.58 us
    ppermute x22 -> x36, waiting for transfers between devices: 60.3 us -> 33.2 us  [swap(): return lax.ppermute(value, AXES, [(d, d ^ mask) for d in range(total)])]
    ppermute x22 -> x36, starting transfers between devices: 28.4 us -> 50 us  [swap(): return lax.ppermute(value, AXES, [(d, d ^ mask) for d in range(total)])]
    pallas_call x2 -> x7, Pallas kernels: 11.9 us -> 30.6 us  [the longest x2 15.6 us: plane(): pl.pallas_call(functools.partial(plane_kernel, frames, widths, rank), in_...]
    add x11 -> x5, other arithmetic: 7.4 us -> 1.52 us  [the longest x1 0.85 us: planes(): jnp.where(core == 0, grams[0], grams[1])]
    ppermute x2 -> x1, waiting for transfers between devices: 5.41 us -> 0.01 us  [planes(): lax.ppermute(edge, 'space', pairs + [(j, i) for i, j in pairs])[:, :, None]]
    dot_general x4 -> x1, matrix products: 6.68 us -> 1.5 us  [planes(): jnp.dot(out_grads.reshape(-1, channels), omega, preferred_element_type=F32)]
    convert_element_type x12 -> x0, local copies, waits for them, and re-layouts: 4.77 us -> none  [the longest x10 4.62 us: halve(): sent = pick(value, 1 - own, axis).astype(BF16)]
    ppermute x2 -> x1, starting transfers between devices: 6.17 us -> 1.46 us  [planes(): lax.ppermute(edge, 'space', pairs + [(j, i) for i, j in pairs])[:, :, None]]
  transfers between devices with their start and end apart: 24 -> 37, of which waited for: 17 -> 14; matrix products, arithmetic and copies ran while one was open for 7% -> 8% of each run, Pallas kernels for 4% -> 22%
where the time goes in v2:
time: 146 us; the launch traced here: 145 us
  starting transfers between devices  51.4 us (35%)
  Pallas kernels  40 us (27%)
  waiting for transfers between devices  33.2 us (23%)
  local copies, waits for them, and re-layouts  12.4 us (8%)
  other arithmetic  6.58 us (5%)
  matrix products  1.5 us (1%)
    ppermute x36, starting transfers between devices, swap(): return lax.ppermute(value, AXES, [(d, d ^ mask) for d in range(total)])  50 us
    ppermute x36, waiting for transfers between devices, swap(): return lax.ppermute(value, AXES, [(d, d ^ mask) for d in range(total)])  33.2 us
    pallas_call x2, Pallas kernels, plane(): pl.pallas_call(functools.partial(plane_kernel, frames, widths, rank), in_...  15.6 us
    pallas_call x1, Pallas kernels, inverse_of_factor(): pl.pallas_call(functools.partial(inverse_kernel, size), out_shape=jax.Sha...  9.42 us
    unnamed x42, local copies, waits for them, and re-layouts  5.78 us
    pallas_call x1, Pallas kernels, basis_of(): pl.pallas_call(functools.partial(basis_kernel, scale), in_specs=[smem, sm...  5.13 us
    pallas_call x2, Pallas kernels, gather(): pl.pallas_call(functools.partial(gather_kernel, rank), in_specs=[pl.Block...  4.93 us
    pallas_call x2, Pallas kernels, turn(): pl.pallas_call(functools.partial(turn_kernel, frames, positions // frames...  4.91 us
  transfers between devices with their start and end apart: 37, of which 14 were waited for; matrix products, arithmetic and copies ran while one was open for 8% of the time, Pallas kernels for 22%

profile of v2, /device:TPU:0, one launch (start us, length us, event | category | flops | bytes accessed | tf_op | source)
XLA Modules:
  0.0 145.5 jit_solution(18027167866700886696)
XLA Ops:
  0.0 1.4 copy-done
  1.4 1.5 %convolution_convert_fusion = bf16[1024,128]{1,0:T(8,128)(2,1)S(1)} fusion(bf16[1024,768]{1,0:T(8,128)(2,1)S(1)} %bitcast.77, bf16[768,128]{1,0:T(8,128)(2,1)} %param.6), kind=kOutput, calls=%fused_computation | convolution fusion | flops 201457664 | bytes 2031616 | tf_op jit(solution)/shard_map/dot_general | solution.py:392
  2.9 1.5 %collective-permute-start.4 = (bf16[2,8,32,128]{3,2,1,0:T(8,128)(2,1)S(1)}, bf16[2,8,32,128]{3,2,1,0:T(8,128)(2,1)}, u32[]{:S(2)}, u32[]{:S(2)}) collective-permute-start(bf16[2,8,32,128]{3,2,1,0:T(8,128)(2,1)S(1)} %fusion.1), channel_id=1, source_target_pairs={{1,2},{3,4},{5,6},{2,1},{4,3},{6,5},{9,10},{11,12},{13,14},{10,9},... | collective-permute-start | bytes 393224 | tf_op jit(solution)/shard_map/ppermute | solution.py:396
  4.4 1.0 maximum_select_fusion
  5.6 9.8 %collective-permute-start.19 = (bf16[8,3,32,128]{3,2,1,0:T(8,128)(2,1)S(1)}, bf16[8,3,32,128]{3,2,1,0:T(8,128)(2,1)S(1)}, u32[]{:S(2)}, u32[]{:S(2)}) collective-permute-start(bf16[8,3,32,128]{3,2,1,0:T(8,128)(2,1)S(1)} %get-tuple-element.51), channel_id=1, source_target_pairs={{0,1},{1,0},{2,3},{3,2},{4,5},{5,4},{6,7},{7,6},{8,9},{9,8},{10,11... | collective-permute-start | bytes 589832 | tf_op jit(solution)/shard_map/ppermute | solution.py:18
  15.4 1.5 %collective-permute-start.20 = (bf16[8,3,32,128]{3,2,1,0:T(8,128)(2,1)S(1)}, bf16[8,3,32,128]{3,2,1,0:T(8,128)(2,1)S(1)}, u32[]{:S(2)}, u32[]{:S(2)}) collective-permute-start(bf16[8,3,32,128]{3,2,1,0:T(8,128)(2,1)S(1)} %get-tuple-element.51), channel_id=1, source_target_pairs={{0,16},{1,17},{2,18},{3,19},{4,20},{5,21},{6,22},{7,23},{8,24},{9,... | collective-permute-start | bytes 589832 | tf_op jit(solution)/shard_map/ppermute | solution.py:18
  17.1 2.0 %collective-permute-start.5 = (bf16[8,3,32,128]{3,2,1,0:T(8,128)(2,1)S(1)}, bf16[8,3,32,128]{3,2,1,0:T(8,128)(2,1)S(1)}, u32[]{:S(2)}, u32[]{:S(2)}) collective-permute-start(bf16[8,3,32,128]{3,2,1,0:T(8,128)(2,1)S(1)} %get-tuple-element.50), channel_id=1, source_target_pairs={{0,1},{1,0},{2,3},{3,2},{4,5},{5,4},{6,7},{7,6},{8,9},{9,8},{10,11... | collective-permute-start | bytes 589832 | tf_op jit(solution)/shard_map/ppermute | solution.py:18
  19.1 1.5 %collective-permute-start.6 = (bf16[8,3,32,128]{3,2,1,0:T(8,128)(2,1)S(1)}, bf16[8,3,32,128]{3,2,1,0:T(8,128)(2,1)S(1)}, u32[]{:S(2)}, u32[]{:S(2)}) collective-permute-start(bf16[8,3,32,128]{3,2,1,0:T(8,128)(2,1)S(1)} %get-tuple-element.50), channel_id=1, source_target_pairs={{0,16},{1,17},{2,18},{3,19},{4,20},{5,21},{6,22},{7,23},{8,24},{9,... | collective-permute-start | bytes 589832 | tf_op jit(solution)/shard_map/ppermute | solution.py:18
  21.0 3.1 %collective-permute-start.7 = (bf16[8,3,32,128]{3,2,1,0:T(8,128)(2,1)S(1)}, bf16[8,3,32,128]{3,2,1,0:T(8,128)(2,1)S(1)}, u32[]{:S(2)}, u32[]{:S(2)}) collective-permute-start(bf16[8,3,32,128]{3,2,1,0:T(8,128)(2,1)S(1)} %get-tuple-element.50), channel_id=1, source_target_pairs={{0,17},{1,16},{2,19},{3,18},{4,21},{5,20},{6,23},{7,22},{8,25},{9,... | collective-permute-start | bytes 589832 | tf_op jit(solution)/shard_map/ppermute | solution.py:18
  24.1 2.9 %collective-permute-done.20 = bf16[8,3,32,128]{3,2,1,0:T(8,128)(2,1)S(1)} collective-permute-done((bf16[8,3,32,128]{3,2,1,0:T(8,128)(2,1)S(1)}, bf16[8,3,32,128]{3,2,1,0:T(8,128)(2,1)S(1)}, u32[]{:S(2)}, u32[]{:S(2)}) %collective-permute-start.20) | collective-permute-done | bytes 196640 | tf_op jit(solution)/shard_map/ppermute | solution.py:18
  27.0 1.0 pad_maximum_fusion.1.own_ref
  28.0 0.8 constant_dynamic-slice_fusion
  29.5 4.2 %collective-permute-done.6 = bf16[8,3,32,128]{3,2,1,0:T(8,128)(2,1)S(1)} collective-permute-done((bf16[8,3,32,128]{3,2,1,0:T(8,128)(2,1)S(1)}, bf16[8,3,32,128]{3,2,1,0:T(8,128)(2,1)S(1)}, u32[]{:S(2)}, u32[]{:S(2)}) %collective-permute-start.6) | collective-permute-done | bytes 196640 | tf_op jit(solution)/shard_map/ppermute | solution.py:18
  33.9 0.7 pad_add_fusion.where_ref
  34.5 0.7 copy-done.11
  35.3 2.4 %turn.3.act_ref = bf16[4,96,1024]{2,1,0:T(8,128)(2,1)} custom-call(s32[3]{0:T(128)} %pad_add_fusion.where_ref, bf16[512,768]{1,0:T(8,128)(2,1)} %bitcast.86, bf16[512,384]{1,0:T(8,128)(2,1)} %copy-done.11), custom_call_target="tpu_custom_call" | custom-call | bytes 1572864 | tf_op jit(solution)/shard_map/turn/pallas_call | solution.py:229
  37.7 1.9 %dynamic-slice_bitcast_fusion = (bf16[96,1024]{1,0:T(8,128)(2,1)}, bf16[96,1024]{1,0:T(8,128)(2,1)}, bf16[96,1024]{1,0:T(8,128)(2,1)}) fusion(bf16[4,96,1024]{2,1,0:T(8,128)(2,1)} %turn.3.act_ref, s32[]{:T(128)S(6)} %select_n.56, s32[]{:T(128)S(6)} %select_n.55, s32[]{:T(128)S(6)} %select_n.54), kind=kLoop, calls=%fused_computation.8 | loop fusion | bytes 1179660 | tf_op jit(solution)/shard_map/jit(dynamic_index_in_dim)/squeeze | solution.py:119
  39.7 1.1 collective-permute-start.16
  41.4 1.7 %collective-permute-start.18 = (bf16[96,1024]{1,0:T(8,128)(2,1)}, bf16[96,1024]{1,0:T(8,128)(2,1)}, u32[]{:S(2)}, u32[]{:S(2)}) collective-permute-start(bf16[96,1024]{1,0:T(8,128)(2,1)} %get-tuple-element.43), channel_id=1, source_target_pairs={{0,17},{1,16},{2,19},{3,18},{4,21},{5,20},{6,23},{7,22},{8,25},{9,... | collective-permute-start | bytes 589832 | tf_op jit(solution)/shard_map/ppermute | solution.py:18
  43.2 0.7 constant_dynamic-slice_fusion.2
  43.9 2.5 %turn.2.act_ref = bf16[4,96,1024]{2,1,0:T(8,128)(2,1)} custom-call(s32[3]{0:T(128)} %pad_add_fusion.where_ref, bf16[512,768]{1,0:T(8,128)(2,1)} %bitcast.84, bf16[512,384]{1,0:T(8,128)(2,1)} %copy-done.10), custom_call_target="tpu_custom_call" | custom-call | bytes 1572864 | tf_op jit(solution)/shard_map/turn/pallas_call | solution.py:229
  46.3 1.2 dynamic-slice_bitcast_fusion.3
  47.6 1.1 collective-permute-start.1
  48.8 0.6 collective-permute-start.2
  49.4 3.4 %collective-permute-done.18.a3 = bf16[96,1024]{1,0:T(8,128)(2,1)} collective-permute-done((bf16[96,1024]{1,0:T(8,128)(2,1)}, bf16[96,1024]{1,0:T(8,128)(2,1)}, u32[]{:S(2)}, u32[]{:S(2)}) %collective-permute-start.18) | collective-permute-done | bytes 196640 | tf_op jit(solution)/shard_map/ppermute | solution.py:18
  52.8 2.2 %collective-permute-start.3 = (bf16[96,1024]{1,0:T(8,128)(2,1)S(1)}, bf16[96,1024]{1,0:T(8,128)(2,1)S(1)}, u32[]{:S(2)}, u32[]{:S(2)}) collective-permute-start(bf16[96,1024]{1,0:T(8,128)(2,1)S(1)} %get-tuple-element.46), channel_id=1, source_target_pairs={{0,17},{1,16},{2,19},{3,18},{4,21},{5,20},{6,23},{7,22},{8,25},{9,... | collective-permute-start | bytes 589832 | tf_op jit(solution)/shard_map/ppermute | solution.py:18
  55.0 8.5 %plane.3 = (f32[28,24,128]{2,1,0:T(8,128)S(1)}, bf16[28,24,128]{2,1,0:T(8,128)(2,1)S(1)}, bf16[28,24,128]{2,1,0:T(8,128)(2,1)}, bf16[28,24,128]{2,1,0:T(8,128)(2,1)}) custom-call(s32[3]{0:T(128)S(1)} %copy-done.6, s32[171]{0:T(256)S(1)} %bitcast.78, bf16[4,96,1024]{2,1,0:T(8,128)(2,1)S(1)} %copy-done.2, bf16[96,1024]{1,0:T(8,128)(2,1)S(1)} %collective-permute-done.16.a1, ...), custom_call_target="tpu_custom_call" | custom-call | flops 2717908992 | bytes 6291456 | tf_op jit(solution)/shard_map/plane/pallas_call | solution.py:292
  63.5 0.7 copy-done.3
  64.2 1.4 collective-permute-start.23
  65.6 1.3 collective-permute-start.24
  66.9 1.7 %collective-permute-start.25 = (bf16[28,24,128]{2,1,0:T(8,128)(2,1)}, bf16[28,24,128]{2,1,0:T(8,128)(2,1)S(1)}, u32[]{:S(2)}, u32[]{:S(2)}) collective-permute-start(bf16[28,24,128]{2,1,0:T(8,128)(2,1)} %get-tuple-element.34), channel_id=1, source_target_pairs={{0,6},{1,7},{2,4},{3,5},{4,2},{5,3},{6,0},{7,1},{8,14},{9,15},{10,... | collective-permute-start | bytes 516104 | tf_op jit(solution)/shard_map/ppermute | solution.py:18
  68.6 7.2 %plane.2 = (f32[28,24,128]{2,1,0:T(8,128)S(1)}, bf16[28,24,128]{2,1,0:T(8,128)(2,1)S(1)}, bf16[28,24,128]{2,1,0:T(8,128)(2,1)S(1)}, bf16[28,24,128]{2,1,0:T(8,128)(2,1)S(1)}) custom-call(s32[3]{0:T(128)S(1)} %copy-done.6, s32[171]{0:T(256)S(1)} %bitcast.79, bf16[4,96,1024]{2,1,0:T(8,128)(2,1)S(1)} %copy-done.1, ...), custom_call_target="tpu_custom_call" | custom-call | flops 2717908992 | bytes 6291456 | tf_op jit(solution)/shard_map/plane/pallas_call | solution.py:292
  75.8 0.7 copy-done.4
  76.6 1.5 %collective-permute-start.10 = (bf16[28,24,128]{2,1,0:T(8,128)(2,1)S(1)}, bf16[28,24,128]{2,1,0:T(8,128)(2,1)S(1)}, u32[]{:S(2)}, u32[]{:S(2)}) collective-permute-start(bf16[28,24,128]{2,1,0:T(8,128)(2,1)S(1)} %get-tuple-element.25), channel_id=1, source_target_pairs={{0,4},{1,5},{2,6},{3,7},{4,0},{5,1},{6,2},{7,3},{8,12},{9,13},{10,... | collective-permute-start | bytes 516104 | tf_op jit(solution)/shard_map/ppermute | solution.py:18
  78.1 1.3 collective-permute-start.11
  80.0 7.3 %collective-permute-done.24.g2 = bf16[28,24,128]{2,1,0:T(8,128)(2,1)S(1)} collective-permute-done((bf16[28,24,128]{2,1,0:T(8,128)(2,1)}, bf16[28,24,128]{2,1,0:T(8,128)(2,1)S(1)}, u32[]{:S(2)}, u32[]{:S(2)}) %collective-permute-start.24) | collective-permute-done | bytes 172064 | tf_op jit(solution)/shard_map/ppermute | solution.py:18
  87.4 0.7 copy-done.15
  88.1 2.5 %gather.3 = (f32[128,128]{1,0:T(8,128)}, f32[2,4,24,128]{3,2,1,0:T(8,128)}, f32[2,4,24,128]{3,2,1,0:T(8,128)}, f32[2,4,24,128]{3,2,1,0:T(8,128)}, f32[2,4,24,128]{3,2,1,0:T(8,128)}) custom-call(s32[171]{0:T(256)} %bitcast.80, f32[28,24,128]{2,1,0:T(8,128)} %copy-done.3, bf16[28,24,128]{2,1,0:T(8,128)(2,1)} %copy-done.14, bf16[28,24,128]{2,1,0:T(8,128)(2,1)} %copy-done.15, ...), custom_call_target="tpu_custom_call" | custom-call | flops 132120576 | bytes 1048576 | tf_op jit(solution)/shard_map/gather/pallas_call | solution.py:329
  90.6 4.2 %collective-permute-done.10.g2 = bf16[28,24,128]{2,1,0:T(8,128)(2,1)S(1)} collective-permute-done((bf16[28,24,128]{2,1,0:T(8,128)(2,1)S(1)}, bf16[28,24,128]{2,1,0:T(8,128)(2,1)S(1)}, u32[]{:S(2)}, u32[]{:S(2)}) %collective-permute-start.10) | collective-permute-done | bytes 172064 | tf_op jit(solution)/shard_map/ppermute | solution.py:18
  94.8 0.7 copy-done.17
  95.6 2.5 %gather.2 = (f32[128,128]{1,0:T(8,128)}, f32[2,4,24,128]{3,2,1,0:T(8,128)}, f32[2,4,24,128]{3,2,1,0:T(8,128)}, f32[2,4,24,128]{3,2,1,0:T(8,128)}, f32[2,4,24,128]{3,2,1,0:T(8,128)}) custom-call(s32[171]{0:T(256)} %bitcast.81, f32[28,24,128]{2,1,0:T(8,128)} %copy-done.4, bf16[28,24,128]{2,1,0:T(8,128)(2,1)} %copy-done.19, bf16[28,24,128]{2,1,0:T(8,128)(2,1)} %copy-done.17, ...), custom_call_target="tpu_custom_call" | custom-call | flops 132120576 | bytes 1048576 | tf_op jit(solution)/shard_map/gather/pallas_call | solution.py:329
  98.0 0.9 broadcast_select_fusion
  99.0 1.0 collective-permute-start.26
  99.9 1.4 collective-permute-start.27
  101.3 1.2 collective-permute-start.28
  102.5 0.8 slice_bitcast_fusion.14
  103.3 1.0 collective-permute-start.12
  104.3 0.8 slice_bitcast_fusion.15
  105.1 1.4 collective-permute-start.13
  106.6 0.9 select_add_fusion
  107.4 1.3 collective-permute-start.14
  108.7 1.0 collective-permute-start.32
  110.1 3.0 %collective-permute-done.32 = f32[128,128]{1,0:T(8,128)S(1)} collective-permute-done((f32[128,128]{1,0:T(8,128)S(1)}, f32[128,128]{1,0:T(8,128)S(1)}, u32[]{:S(2)}, u32[]{:S(2)}) %collective-permute-start.32) | collective-permute-done | bytes 65568 | tf_op jit(solution)/shard_map/ppermute | solution.py:18
  113.1 1.4 collective-permute-start.33
  114.6 2.9 %collective-permute-done.33 = f32[128,128]{1,0:T(8,128)S(1)} collective-permute-done((f32[128,128]{1,0:T(8,128)S(1)}, f32[128,128]{1,0:T(8,128)S(1)}, u32[]{:S(2)}, u32[]{:S(2)}) %collective-permute-start.33) | collective-permute-done | bytes 65568 | tf_op jit(solution)/shard_map/ppermute | solution.py:18
  117.5 2.5 %collective-permute-start.34 = (f32[128,128]{1,0:T(8,128)S(1)}, f32[128,128]{1,0:T(8,128)S(1)}, u32[]{:S(2)}, u32[]{:S(2)}) collective-permute-start(f32[128,128]{1,0:T(8,128)S(1)} %add.51), channel_id=1, source_target_pairs={{0,2},{1,3},{2,0},{3,1},{4,6},{5,7},{6,4},{7,5},{8,10},{9,11},{10,... | collective-permute-start | bytes 196616 | tf_op jit(solution)/shard_map/ppermute | solution.py:18
  120.0 2.1 %collective-permute-done.34 = f32[128,128]{1,0:T(8,128)S(1)} collective-permute-done((f32[128,128]{1,0:T(8,128)S(1)}, f32[128,128]{1,0:T(8,128)S(1)}, u32[]{:S(2)}, u32[]{:S(2)}) %collective-permute-start.34) | collective-permute-done | bytes 65568 | tf_op jit(solution)/shard_map/ppermute | solution.py:18
  122.2 3.7 %collective-permute-start.35 = (f32[128,128]{1,0:T(8,128)S(1)}, f32[128,128]{1,0:T(8,128)S(1)}, u32[]{:S(2)}, u32[]{:S(2)}) collective-permute-start(f32[128,128]{1,0:T(8,128)S(1)} %add.52), channel_id=1, source_target_pairs={{0,4},{1,5},{2,6},{3,7},{4,0},{5,1},{6,2},{7,3},{8,12},{9,13},{10,... | collective-permute-start | bytes 196616 | tf_op jit(solution)/shard_map/ppermute | solution.py:18
  125.9 0.7 pad_maximum_fusion.3.own1
  126.6 1.5 %collective-permute-done.35 = f32[128,128]{1,0:T(8,128)S(1)} collective-permute-done((f32[128,128]{1,0:T(8,128)S(1)}, f32[128,128]{1,0:T(8,128)S(1)}, u32[]{:S(2)}, u32[]{:S(2)}) %collective-permute-start.35) | collective-permute-done | bytes 65568 | tf_op jit(solution)/shard_map/ppermute | solution.py:18
  128.8 9.4 %inverse.1.mine_ref = f32[128,128]{1,0:T(8,128)} custom-call(f32[128,128]{1,0:T(8,128)} %add.53.gram_ref), custom_call_target="tpu_custom_call" | custom-call | tf_op jit(solution)/shard_map/inverse/pallas_call | solution.py:110
  138.2 0.7 pad_maximum_fusion.2.own0
  139.0 0.8 collective-permute-done.36.theirs_ref
  140.3 5.1 %basis.1 = f32[2,648,128]{2,1,0:T(8,128)} custom-call(s32[3]{0:T(128)} %pad_add_fusion.where_ref, s32[171]{0:T(256)} %bitcast.82, f32[16,24,128]{2,1,0:T(8,128)} %pad_maximum_fusion.2.own0, f32[16,24,128]{2,1,0:T(8,128)} %pad_maximum_fusion.3.own1, f32[16,24,128]{2,1,0:T(8,128)} %copy-done.13, f32[16,24,128]{2,1,0:T(8,128)} %copy-done.12, ...), custom_call_target="tpu_custom_call" | custom-call | tf_op jit(solution)/shard_map/basis/pallas_call | solution.py:365
  (91 shorter events, 5.1 us)
Async XLA Ops:
  0.0 1.4 copy-start
  2.9 14.0 %copy-start.9 = (bf16[2,1,8,2,32,768]{5,4,3,2,1,0:T(8,128)(2,1)S(1)}, bf16[2,1,8,2,32,768]{5,4,3,2,1,0:T(8,128)(2,1)}, u32[]{:S(2)}) copy-start(bf16[2,1,8,2,32,768]{5,4,3,2,1,0:T(8,128)(2,1)} %param.4) | copy-start | bytes 4718596
  2.9 1.5 %collective-permute-start.4 = (bf16[2,8,32,128]{3,2,1,0:T(8,128)(2,1)S(1)}, bf16[2,8,32,128]{3,2,1,0:T(8,128)(2,1)}, u32[]{:S(2)}, u32[]{:S(2)}) collective-permute-start(bf16[2,8,32,128]{3,2,1,0:T(8,128)(2,1)S(1)} %fusion.1), channel_id=1, source_target_pairs={{1,2},{3,4},{5,6},{2,1},{4,3},{6,5},{9,10},{11,12},{13,14},{10,9},... | collective-permute-start | bytes 393224 | tf_op jit(solution)/shard_map/ppermute | solution.py:396
  5.6 15.5 %collective-permute-start.19 = (bf16[8,3,32,128]{3,2,1,0:T(8,128)(2,1)S(1)}, bf16[8,3,32,128]{3,2,1,0:T(8,128)(2,1)S(1)}, u32[]{:S(2)}, u32[]{:S(2)}) collective-permute-start(bf16[8,3,32,128]{3,2,1,0:T(8,128)(2,1)S(1)} %get-tuple-element.51), channel_id=1, source_target_pairs={{0,1},{1,0},{2,3},{3,2},{4,5},{5,4},{6,7},{7,6},{8,9},{9,8},{10,11... | collective-permute-start | bytes 589832 | tf_op jit(solution)/shard_map/ppermute | solution.py:18
  15.4 11.6 %collective-permute-start.20 = (bf16[8,3,32,128]{3,2,1,0:T(8,128)(2,1)S(1)}, bf16[8,3,32,128]{3,2,1,0:T(8,128)(2,1)S(1)}, u32[]{:S(2)}, u32[]{:S(2)}) collective-permute-start(bf16[8,3,32,128]{3,2,1,0:T(8,128)(2,1)S(1)} %get-tuple-element.51), channel_id=1, source_target_pairs={{0,16},{1,17},{2,18},{3,19},{4,20},{5,21},{6,22},{7,23},{8,24},{9,... | collective-permute-start | bytes 589832 | tf_op jit(solution)/shard_map/ppermute | solution.py:18
  16.9 10.1 %collective-permute-start.21 = (bf16[8,3,32,128]{3,2,1,0:T(8,128)(2,1)S(1)}, bf16[8,3,32,128]{3,2,1,0:T(8,128)(2,1)S(1)}, u32[]{:S(2)}, u32[]{:S(2)}) collective-permute-start(bf16[8,3,32,128]{3,2,1,0:T(8,128)(2,1)S(1)} %get-tuple-element.51), channel_id=1, source_target_pairs={{0,17},{1,16},{2,19},{3,18},{4,21},{5,20},{6,23},{7,22},{8,25},{9,... | collective-permute-start | bytes 589832 | tf_op jit(solution)/shard_map/ppermute | solution.py:18
  17.1 12.3 %copy-start.7 = (bf16[1,1,8,2,32,768]{5,4,3,2,1,0:T(8,128)(2,1)}, bf16[1,1,8,2,32,768]{5,4,3,2,1,0:T(8,128)(2,1)S(1)}, u32[]{:S(2)}) copy-start(bf16[1,1,8,2,32,768]{5,4,3,2,1,0:T(8,128)(2,1)S(1)} %get-tuple-element.42) | copy-start | bytes 2359300
  17.1 12.3 %copy-start.8 = (bf16[1,1,8,2,32,768]{5,4,3,2,1,0:T(8,128)(2,1)}, bf16[1,1,8,2,32,768]{5,4,3,2,1,0:T(8,128)(2,1)S(1)}, u32[]{:S(2)}) copy-start(bf16[1,1,8,2,32,768]{5,4,3,2,1,0:T(8,128)(2,1)S(1)} %get-tuple-element.41) | copy-start | bytes 2359300
  17.1 12.4 %collective-permute-start.5 = (bf16[8,3,32,128]{3,2,1,0:T(8,128)(2,1)S(1)}, bf16[8,3,32,128]{3,2,1,0:T(8,128)(2,1)S(1)}, u32[]{:S(2)}, u32[]{:S(2)}) collective-permute-start(bf16[8,3,32,128]{3,2,1,0:T(8,128)(2,1)S(1)} %get-tuple-element.50), channel_id=1, source_target_pairs={{0,1},{1,0},{2,3},{3,2},{4,5},{5,4},{6,7},{7,6},{8,9},{9,8},{10,11... | collective-permute-start | bytes 589832 | tf_op jit(solution)/shard_map/ppermute | solution.py:18
  19.1 14.5 %collective-permute-start.6 = (bf16[8,3,32,128]{3,2,1,0:T(8,128)(2,1)S(1)}, bf16[8,3,32,128]{3,2,1,0:T(8,128)(2,1)S(1)}, u32[]{:S(2)}, u32[]{:S(2)}) collective-permute-start(bf16[8,3,32,128]{3,2,1,0:T(8,128)(2,1)S(1)} %get-tuple-element.50), channel_id=1, source_target_pairs={{0,16},{1,17},{2,18},{3,19},{4,20},{5,21},{6,22},{7,23},{8,24},{9,... | collective-permute-start | bytes 589832 | tf_op jit(solution)/shard_map/ppermute | solution.py:18
  21.0 12.6 %collective-permute-start.7 = (bf16[8,3,32,128]{3,2,1,0:T(8,128)(2,1)S(1)}, bf16[8,3,32,128]{3,2,1,0:T(8,128)(2,1)S(1)}, u32[]{:S(2)}, u32[]{:S(2)}) collective-permute-start(bf16[8,3,32,128]{3,2,1,0:T(8,128)(2,1)S(1)} %get-tuple-element.50), channel_id=1, source_target_pairs={{0,17},{1,16},{2,19},{3,18},{4,21},{5,20},{6,23},{7,22},{8,25},{9,... | collective-permute-start | bytes 589832 | tf_op jit(solution)/shard_map/ppermute | solution.py:18
  28.0 27.0 %collective-permute-start.22 = (bf16[4,8,3,32,128]{4,3,2,1,0:T(8,128)(2,1)}, bf16[4,8,3,32,128]{4,3,2,1,0:T(8,128)(2,1)}, u32[]{:S(2)}, u32[]{:S(2)}) collective-permute-start(bf16[4,8,3,32,128]{4,3,2,1,0:T(8,128)(2,1)} %pad_maximum_fusion.1.own_ref), channel_id=1, source_target_pairs={{0,8},{1,9},{2,10},{3,11},{4,12},{5,13},{6,14},{7,15},{8,0},{9,1},... | collective-permute-start | bytes 2359304 | tf_op jit(solution)/shard_map/ppermute | solution.py:18
  28.8 5.7 %collective-permute-start.15 = (bf16[512,384]{1,0:T(8,128)(2,1)}, bf16[512,384]{1,0:T(8,128)(2,1)S(1)}, u32[]{:S(2)}, u32[]{:S(2)}) collective-permute-start(bf16[512,384]{1,0:T(8,128)(2,1)} %constant_dynamic-slice_fusion), channel_id=1, source_target_pairs={{0,8},{1,9},{2,10},{3,11},{4,12},{5,13},{6,14},{7,15},{8,0},{9,1},... | collective-permute-start | bytes 1179656 | tf_op jit(solution)/shard_map/ppermute | solution.py:18
  29.5 11.9 %collective-permute-start = (bf16[512,384]{1,0:T(8,128)(2,1)S(1)}, bf16[512,384]{1,0:T(8,128)(2,1)S(1)}, u32[]{:S(2)}, u32[]{:S(2)}) collective-permute-start(bf16[512,384]{1,0:T(8,128)(2,1)S(1)} %constant_dynamic-slice_fusion.1), channel_id=1, source_target_pairs={{0,8},{1,9},{2,10},{3,11},{4,12},{5,13},{6,14},{7,15},{8,0},{9,1},... | collective-permute-start | bytes 1179656 | tf_op jit(solution)/shard_map/ppermute | solution.py:18
  33.8 34.9 %collective-permute-start.8 = (bf16[4,8,3,32,128]{4,3,2,1,0:T(8,128)(2,1)S(1)}, bf16[4,8,3,32,128]{4,3,2,1,0:T(8,128)(2,1)}, u32[]{:S(2)}, u32[]{:S(2)}) collective-permute-start(bf16[4,8,3,32,128]{4,3,2,1,0:T(8,128)(2,1)S(1)} %pad_maximum_fusion.own_ref), channel_id=1, source_target_pairs={{0,8},{1,9},{2,10},{3,11},{4,12},{5,13},{6,14},{7,15},{8,0},{9,1},... | collective-permute-start | bytes 2359304 | tf_op jit(solution)/shard_map/ppermute | solution.py:18
  34.5 0.7 copy-start.11
  39.7 8.0 %collective-permute-start.16 = (bf16[96,1024]{1,0:T(8,128)(2,1)}, bf16[96,1024]{1,0:T(8,128)(2,1)S(1)}, u32[]{:S(2)}, u32[]{:S(2)}) collective-permute-start(bf16[96,1024]{1,0:T(8,128)(2,1)} %get-tuple-element.45), channel_id=1, source_target_pairs={{0,1},{1,0},{2,3},{3,2},{4,5},{5,4},{6,7},{7,6},{8,9},{9,8},{10,11... | collective-permute-start | bytes 589832 | tf_op jit(solution)/shard_map/ppermute | solution.py:18
  40.8 8.0 %collective-permute-start.17 = (bf16[96,1024]{1,0:T(8,128)(2,1)}, bf16[96,1024]{1,0:T(8,128)(2,1)S(1)}, u32[]{:S(2)}, u32[]{:S(2)}) collective-permute-start(bf16[96,1024]{1,0:T(8,128)(2,1)} %get-tuple-element.44), channel_id=1, source_target_pairs={{0,16},{1,17},{2,18},{3,19},{4,20},{5,21},{6,22},{7,23},{8,24},{9,... | collective-permute-start | bytes 589832 | tf_op jit(solution)/shard_map/ppermute | solution.py:18
  41.4 1.7 %copy-start.10 = (bf16[512,384]{1,0:T(8,128)(2,1)}, bf16[512,384]{1,0:T(8,128)(2,1)S(1)}, u32[]{:S(2)}) copy-start(bf16[512,384]{1,0:T(8,128)(2,1)S(1)} %collective-permute-done.got_ref) | copy-start | bytes 1179652
  41.4 11.4 %collective-permute-start.18 = (bf16[96,1024]{1,0:T(8,128)(2,1)}, bf16[96,1024]{1,0:T(8,128)(2,1)}, u32[]{:S(2)}, u32[]{:S(2)}) collective-permute-start(bf16[96,1024]{1,0:T(8,128)(2,1)} %get-tuple-element.43), channel_id=1, source_target_pairs={{0,17},{1,16},{2,19},{3,18},{4,21},{5,20},{6,23},{7,22},{8,25},{9,... | collective-permute-start | bytes 589832 | tf_op jit(solution)/shard_map/ppermute | solution.py:18
  43.9 24.8 %copy-start.5 = (s32[1,171]{1,0:T(1,128)}, s32[1,171]{1,0:T(1,128)S(1)}, u32[]{:S(2)}) copy-start(s32[1,171]{1,0:T(1,128)S(1)} %constant_dynamic-slice_fusion.2) | copy-start | bytes 2056
  43.9 11.1 %copy-start.2 = (bf16[4,96,1024]{2,1,0:T(8,128)(2,1)S(1)}, bf16[4,96,1024]{2,1,0:T(8,128)(2,1)}, u32[]{:S(2)}) copy-start(bf16[4,96,1024]{2,1,0:T(8,128)(2,1)} %turn.3.act_ref) | copy-start | bytes 2359300
  43.9 11.1 %copy-start.6 = (s32[3]{0:T(128)S(1)}, s32[3]{0:T(128)}, u32[]{:S(2)}) copy-start(s32[3]{0:T(128)} %pad_add_fusion.where_ref) | copy-start | bytes 40
  47.6 18.0 %collective-permute-start.1 = (bf16[96,1024]{1,0:T(8,128)(2,1)S(1)}, bf16[96,1024]{1,0:T(8,128)(2,1)S(1)}, u32[]{:S(2)}, u32[]{:S(2)}) collective-permute-start(bf16[96,1024]{1,0:T(8,128)(2,1)S(1)} %get-tuple-element.48), channel_id=1, source_target_pairs={{0,1},{1,0},{2,3},{3,2},{4,5},{5,4},{6,7},{7,6},{8,9},{9,8},{10,11... | collective-permute-start | bytes 589832 | tf_op jit(solution)/shard_map/ppermute | solution.py:18
  48.8 18.1 %collective-permute-start.2 = (bf16[96,1024]{1,0:T(8,128)(2,1)S(1)}, bf16[96,1024]{1,0:T(8,128)(2,1)S(1)}, u32[]{:S(2)}, u32[]{:S(2)}) collective-permute-start(bf16[96,1024]{1,0:T(8,128)(2,1)S(1)} %get-tuple-element.47), channel_id=1, source_target_pairs={{0,16},{1,17},{2,18},{3,19},{4,20},{5,21},{6,22},{7,23},{8,24},{9,... | collective-permute-start | bytes 589832 | tf_op jit(solution)/shard_map/ppermute | solution.py:18
  52.8 15.8 %collective-permute-start.3 = (bf16[96,1024]{1,0:T(8,128)(2,1)S(1)}, bf16[96,1024]{1,0:T(8,128)(2,1)S(1)}, u32[]{:S(2)}, u32[]{:S(2)}) collective-permute-start(bf16[96,1024]{1,0:T(8,128)(2,1)S(1)} %get-tuple-element.46), channel_id=1, source_target_pairs={{0,17},{1,16},{2,19},{3,18},{4,21},{5,20},{6,23},{7,22},{8,25},{9,... | collective-permute-start | bytes 589832 | tf_op jit(solution)/shard_map/ppermute | solution.py:18
  55.0 13.6 %copy-start.1 = (bf16[4,96,1024]{2,1,0:T(8,128)(2,1)S(1)}, bf16[4,96,1024]{2,1,0:T(8,128)(2,1)}, u32[]{:S(2)}) copy-start(bf16[4,96,1024]{2,1,0:T(8,128)(2,1)} %turn.2.act_ref) | copy-start | bytes 2359300
  63.5 0.7 copy-start.3
  64.2 15.2 %collective-permute-start.23 = (bf16[28,24,128]{2,1,0:T(8,128)(2,1)S(1)}, bf16[28,24,128]{2,1,0:T(8,128)(2,1)S(1)}, u32[]{:S(2)}, u32[]{:S(2)}) collective-permute-start(bf16[28,24,128]{2,1,0:T(8,128)(2,1)S(1)} %get-tuple-element.32), channel_id=1, source_target_pairs={{0,2},{1,3},{2,0},{3,1},{4,6},{5,7},{6,4},{7,5},{8,10},{9,11},{10,... | collective-permute-start | bytes 516104 | tf_op jit(solution)/shard_map/ppermute | solution.py:18
  65.6 21.8 %collective-permute-start.24 = (bf16[28,24,128]{2,1,0:T(8,128)(2,1)}, bf16[28,24,128]{2,1,0:T(8,128)(2,1)S(1)}, u32[]{:S(2)}, u32[]{:S(2)}) collective-permute-start(bf16[28,24,128]{2,1,0:T(8,128)(2,1)} %get-tuple-element.33), channel_id=1, source_target_pairs={{0,4},{1,5},{2,6},{3,7},{4,0},{5,1},{6,2},{7,3},{8,12},{9,13},{10,... | collective-permute-start | bytes 516104 | tf_op jit(solution)/shard_map/ppermute | solution.py:18
  66.9 20.5 %collective-permute-start.25 = (bf16[28,24,128]{2,1,0:T(8,128)(2,1)}, bf16[28,24,128]{2,1,0:T(8,128)(2,1)S(1)}, u32[]{:S(2)}, u32[]{:S(2)}) collective-permute-start(bf16[28,24,128]{2,1,0:T(8,128)(2,1)} %get-tuple-element.34), channel_id=1, source_target_pairs={{0,6},{1,7},{2,4},{3,5},{4,2},{5,3},{6,0},{7,1},{8,14},{9,15},{10,... | collective-permute-start | bytes 516104 | tf_op jit(solution)/shard_map/ppermute | solution.py:18
  75.8 0.7 copy-start.4
  76.6 18.2 %collective-permute-start.10 = (bf16[28,24,128]{2,1,0:T(8,128)(2,1)S(1)}, bf16[28,24,128]{2,1,0:T(8,128)(2,1)S(1)}, u32[]{:S(2)}, u32[]{:S(2)}) collective-permute-start(bf16[28,24,128]{2,1,0:T(8,128)(2,1)S(1)} %get-tuple-element.25), channel_id=1, source_target_pairs={{0,4},{1,5},{2,6},{3,7},{4,0},{5,1},{6,2},{7,3},{8,12},{9,13},{10,... | collective-permute-start | bytes 516104 | tf_op jit(solution)/shard_map/ppermute | solution.py:18
  78.1 16.7 %collective-permute-start.11 = (bf16[28,24,128]{2,1,0:T(8,128)(2,1)S(1)}, bf16[28,24,128]{2,1,0:T(8,128)(2,1)S(1)}, u32[]{:S(2)}, u32[]{:S(2)}) collective-permute-start(bf16[28,24,128]{2,1,0:T(8,128)(2,1)S(1)} %get-tuple-element.26), channel_id=1, source_target_pairs={{0,6},{1,7},{2,4},{3,5},{4,2},{5,3},{6,0},{7,1},{8,14},{9,15},{10,... | collective-permute-start | bytes 516104 | tf_op jit(solution)/shard_map/ppermute | solution.py:18
  79.4 8.0 %copy-start.14 = (bf16[28,24,128]{2,1,0:T(8,128)(2,1)}, bf16[28,24,128]{2,1,0:T(8,128)(2,1)S(1)}, u32[]{:S(2)}) copy-start(bf16[28,24,128]{2,1,0:T(8,128)(2,1)S(1)} %collective-permute-done.23.g1) | copy-start | bytes 516100
  79.4 15.4 %collective-permute-start.9 = (bf16[28,24,128]{2,1,0:T(8,128)(2,1)S(1)}, bf16[28,24,128]{2,1,0:T(8,128)(2,1)S(1)}, u32[]{:S(2)}, u32[]{:S(2)}) collective-permute-start(bf16[28,24,128]{2,1,0:T(8,128)(2,1)S(1)} %get-tuple-element.24), channel_id=1, source_target_pairs={{0,2},{1,3},{2,0},{3,1},{4,6},{5,7},{6,4},{7,5},{8,10},{9,11},{10,... | collective-permute-start | bytes 516104 | tf_op jit(solution)/shard_map/ppermute | solution.py:18
  87.4 0.7 copy-start.15
  87.4 0.7 copy-start.16
  94.8 0.7 copy-start.17
  94.8 0.7 copy-start.18
  94.8 0.8 copy-start.19
  98.9 6.3 %collective-permute-start.31 = (f32[128,128]{1,0:T(8,128)S(1)}, f32[128,128]{1,0:T(8,128)S(1)}, u32[]{:S(2)}, u32[]{:S(2)}) collective-permute-start(f32[128,128]{1,0:T(8,128)S(1)} %broadcast_select_fusion), channel_id=1, source_target_pairs={{0,8},{1,9},{2,10},{3,11},{4,12},{5,13},{6,14},{7,15},{8,0},{9,1},... | collective-permute-start | bytes 196616 | tf_op jit(solution)/shard_map/ppermute | solution.py:18
  99.0 8.5 %collective-permute-start.26 = (f32[2,4,24,128]{3,2,1,0:T(8,128)}, f32[2,4,24,128]{3,2,1,0:T(8,128)S(1)}, u32[]{:S(2)}, u32[]{:S(2)}) collective-permute-start(f32[2,4,24,128]{3,2,1,0:T(8,128)} %get-tuple-element.36), channel_id=1, source_target_pairs={{0,1},{1,0},{2,3},{3,2},{4,5},{5,4},{6,7},{7,6},{8,9},{9,8},{10,11... | collective-permute-start | bytes 294920 | tf_op jit(solution)/shard_map/ppermute | solution.py:18
  99.9 8.8 %collective-permute-start.27 = (f32[2,4,24,128]{3,2,1,0:T(8,128)}, f32[2,4,24,128]{3,2,1,0:T(8,128)S(1)}, u32[]{:S(2)}, u32[]{:S(2)}) collective-permute-start(f32[2,4,24,128]{3,2,1,0:T(8,128)} %get-tuple-element.37), channel_id=1, source_target_pairs={{0,16},{1,17},{2,18},{3,19},{4,20},{5,21},{6,22},{7,23},{8,24},{9,... | collective-permute-start | bytes 294920 | tf_op jit(solution)/shard_map/ppermute | solution.py:18
  101.3 8.4 %collective-permute-start.28 = (f32[2,4,24,128]{3,2,1,0:T(8,128)}, f32[2,4,24,128]{3,2,1,0:T(8,128)S(1)}, u32[]{:S(2)}, u32[]{:S(2)}) collective-permute-start(f32[2,4,24,128]{3,2,1,0:T(8,128)} %get-tuple-element.38), channel_id=1, source_target_pairs={{0,17},{1,16},{2,19},{3,18},{4,21},{5,20},{6,23},{7,22},{8,25},{9,... | collective-permute-start | bytes 294920 | tf_op jit(solution)/shard_map/ppermute | solution.py:18
  103.3 6.5 %collective-permute-start.12 = (f32[2,4,24,128]{3,2,1,0:T(8,128)}, f32[2,4,24,128]{3,2,1,0:T(8,128)S(1)}, u32[]{:S(2)}, u32[]{:S(2)}) collective-permute-start(f32[2,4,24,128]{3,2,1,0:T(8,128)} %get-tuple-element.28), channel_id=1, source_target_pairs={{0,1},{1,0},{2,3},{3,2},{4,5},{5,4},{6,7},{7,6},{8,9},{9,8},{10,11... | collective-permute-start | bytes 294920 | tf_op jit(solution)/shard_map/ppermute | solution.py:18
  105.1 5.0 %collective-permute-start.13 = (f32[2,4,24,128]{3,2,1,0:T(8,128)}, f32[2,4,24,128]{3,2,1,0:T(8,128)S(1)}, u32[]{:S(2)}, u32[]{:S(2)}) collective-permute-start(f32[2,4,24,128]{3,2,1,0:T(8,128)} %get-tuple-element.29), channel_id=1, source_target_pairs={{0,16},{1,17},{2,18},{3,19},{4,20},{5,21},{6,22},{7,23},{8,24},{9,... | collective-permute-start | bytes 294920 | tf_op jit(solution)/shard_map/ppermute | solution.py:18
  107.4 7.1 %collective-permute-start.14 = (f32[2,4,24,128]{3,2,1,0:T(8,128)}, f32[2,4,24,128]{3,2,1,0:T(8,128)S(1)}, u32[]{:S(2)}, u32[]{:S(2)}) collective-permute-start(f32[2,4,24,128]{3,2,1,0:T(8,128)} %get-tuple-element.30), channel_id=1, source_target_pairs={{0,17},{1,16},{2,19},{3,18},{4,21},{5,20},{6,23},{7,22},{8,25},{9,... | collective-permute-start | bytes 294920 | tf_op jit(solution)/shard_map/ppermute | solution.py:18
  108.7 4.4 %collective-permute-start.32 = (f32[128,128]{1,0:T(8,128)S(1)}, f32[128,128]{1,0:T(8,128)S(1)}, u32[]{:S(2)}, u32[]{:S(2)}) collective-permute-start(f32[128,128]{1,0:T(8,128)S(1)} %select_add_fusion), channel_id=1, source_target_pairs={{0,1},{1,0},{2,3},{3,2},{4,5},{5,4},{6,7},{7,6},{8,9},{9,8},{10,11... | collective-permute-start | bytes 196616 | tf_op jit(solution)/shard_map/ppermute | solution.py:18
  109.8 29.2 %collective-permute-start.30 = (f32[16,24,128]{2,1,0:T(8,128)S(1)}, f32[16,24,128]{2,1,0:T(8,128)S(1)}, u32[]{:S(2)}, u32[]{:S(2)}) collective-permute-start(f32[16,24,128]{2,1,0:T(8,128)S(1)} %pad_maximum_fusion.5), channel_id=1, source_target_pairs={{0,8},{1,9},{2,10},{3,11},{4,12},{5,13},{6,14},{7,15},{8,0},{9,1},... | collective-permute-start | bytes 589832 | tf_op jit(solution)/shard_map/ppermute | solution.py:18
  113.1 4.3 %collective-permute-start.33 = (f32[128,128]{1,0:T(8,128)S(1)}, f32[128,128]{1,0:T(8,128)S(1)}, u32[]{:S(2)}, u32[]{:S(2)}) collective-permute-start(f32[128,128]{1,0:T(8,128)S(1)} %add.50), channel_id=1, source_target_pairs={{0,16},{1,17},{2,18},{3,19},{4,20},{5,21},{6,22},{7,23},{8,24},{9,... | collective-permute-start | bytes 196616 | tf_op jit(solution)/shard_map/ppermute | solution.py:18
  117.5 4.7 %collective-permute-start.34 = (f32[128,128]{1,0:T(8,128)S(1)}, f32[128,128]{1,0:T(8,128)S(1)}, u32[]{:S(2)}, u32[]{:S(2)}) collective-permute-start(f32[128,128]{1,0:T(8,128)S(1)} %add.51), channel_id=1, source_target_pairs={{0,2},{1,3},{2,0},{3,1},{4,6},{5,7},{6,4},{7,5},{8,10},{9,11},{10,... | collective-permute-start | bytes 196616 | tf_op jit(solution)/shard_map/ppermute | solution.py:18
  119.9 19.0 %collective-permute-start.29 = (f32[16,24,128]{2,1,0:T(8,128)S(1)}, f32[16,24,128]{2,1,0:T(8,128)S(1)}, u32[]{:S(2)}, u32[]{:S(2)}) collective-permute-start(f32[16,24,128]{2,1,0:T(8,128)S(1)} %pad_maximum_fusion.4), channel_id=1, source_target_pairs={{0,8},{1,9},{2,10},{3,11},{4,12},{5,13},{6,14},{7,15},{8,0},{9,1},... | collective-permute-start | bytes 589832 | tf_op jit(solution)/shard_map/ppermute | solution.py:18
  122.2 6.0 %collective-permute-start.35 = (f32[128,128]{1,0:T(8,128)S(1)}, f32[128,128]{1,0:T(8,128)S(1)}, u32[]{:S(2)}, u32[]{:S(2)}) collective-permute-start(f32[128,128]{1,0:T(8,128)S(1)} %add.52), channel_id=1, source_target_pairs={{0,4},{1,5},{2,6},{3,7},{4,0},{5,1},{6,2},{7,3},{8,12},{9,13},{10,... | collective-permute-start | bytes 196616 | tf_op jit(solution)/shard_map/ppermute | solution.py:18
  138.2 1.5 %collective-permute-start.36 = (f32[128,128]{1,0:T(8,128)}, f32[128,128]{1,0:T(8,128)S(1)}, u32[]{:S(2)}, u32[]{:S(2)}) collective-permute-start(f32[128,128]{1,0:T(8,128)} %inverse.1.mine_ref), channel_id=1, source_target_pairs={{0,8},{1,9},{2,10},{3,11},{4,12},{5,13},{6,14},{7,15},{8,0},{9,1},... | collective-permute-start | bytes 196616 | tf_op jit(solution)/shard_map/ppermute | solution.py:18
  138.9 0.8 copy-start.12
  138.9 0.8 copy-start.13
  139.7 0.6 copy-start.20
